TPU v7x, 32 devices: a whole 2x2x4 slice. The times are simulated.
32 devices in a mesh: fsdp: 8 (over z, y), ctx: 2 (over x), tp: 2 (over core).
Axes of the slice: x: 2, y: 2, z: 4, core: 2. Of those that a mesh axis runs over, the one named last changes fastest.
Arguments:
- tokens: bfloat16 [8, 2, 1280, 768], P('fsdp', 'ctx'), may hold values from -6 to 6
- cotangent: bfloat16 [8, 2, 1280, 768], P('fsdp', 'ctx'), may hold values from -6 to 6
- routes: int32 [8, 2, 1280, 1], P('fsdp', 'ctx', 'tp'), may hold values from 0 to 15; in each aligned block of 640 rows (0 to 639, 640 to 1279, ..., all dimensions but the last counted through in order) at most 80 rows name the same one
- qkv_weight: bfloat16 [3, 768, 768], P(None, 'fsdp', 'tp'), may hold values from -0.3125 to 0.3125
- out_weight: bfloat16 [768, 768], P('tp', 'fsdp'), may hold values from -0.625 to 0.625
- layer_norm_gains: float32 [2, 768], replicated, may hold values from 0.5 to 1.5
- layer_norm_biases: float32 [2, 768], replicated, may hold values from -2 to 2
- up_weight: bfloat16 [16, 768, 3072], P('fsdp', ('ctx', 'tp')), may hold values from -0.21875 to 0.21875
- up_shift: bfloat16 [16, 3072], P('fsdp', ('ctx', 'tp')), may hold values from -2 to 2
- down_weight: bfloat16 [16, 3072, 768], P('fsdp', ('ctx', 'tp')), may hold values from -0.3125 to 0.3125
- down_shift: bfloat16 [16, 768], P('fsdp', ('ctx', 'tp')), may hold values from -2 to 2
- centroids: bfloat16 [16, 768], P('fsdp', ('ctx', 'tp')), may hold values from -0.15625 to 0.15625
Outputs:
- mixed: bfloat16 [8, 2, 1280, 768], P('fsdp', 'ctx')
- tokens_grad: float32 [8, 2, 1280, 768], P('fsdp', 'ctx')
- qkv_grad: float32 [3, 768, 768], P(None, ('fsdp', 'ctx'), 'tp')
- out_grad: float32 [768, 768], P('tp', ('fsdp', 'ctx'))
- gains_grad: float32 [2, 768], P(None, ('fsdp', 'ctx'))
- shifts_grad: float32 [2, 768], P(None, ('fsdp', 'ctx'))
- up_grad: float32 [16, 768, 3072], P('fsdp', ('ctx', 'tp'))
- up_shift_grad: float32 [16, 3072], P('fsdp', ('ctx', 'tp'))
- down_grad: float32 [16, 3072, 768], P('fsdp', ('ctx', 'tp'))
- down_shift_grad: float32 [16, 768], P('fsdp', ('ctx', 'tp'))
- centroids_grad: float32 [16, 768], P('fsdp', ('ctx', 'tp'))
Inputs may be any that keep to these rules, and one draw needn't show every extreme that they name: `routes`: in each aligned block of 640 tokens (the tokens of dimension 2 taken in halves of a block, in order), no expert is named more than 80 times, a bound that some block reaches.
All inputs are finite; a program needn't handle non-finite values.
Results may differ from a plain program's by a relative error of at most 0.024.
Values may be sent and summed in bfloat16 or wider, within the bound.
No kernel may reach another device: no remote copies, remote signals or barrier semaphores. Data moves between devices by JAX's collectives and lax.ppermute only.
A program may use at most 256 MiB of HBM per device.

v0:
```python
from functools import partial

import jax
import jax.numpy as jnp
from jax import lax
from jax.sharding import PartitionSpec as P

HEAD_DIM = 64
PROMPT = 2048
LEN = 256


EPS = 1e-05
NEG = -1e30


def norm_input_rows(values, gain, shift):
    mean = jnp.mean(values, axis=-1, keepdims=True)
    centred = values - mean
    spread = lax.rsqrt(jnp.mean(centred * centred, axis=-1, keepdims=True) + EPS)
    normed = centred * spread
    return (normed * gain + shift, normed, spread)


def norm_back(upstream, normed, spread, gain):
    scaled = upstream * gain
    inner = (
        scaled
        - jnp.mean(scaled, axis=-1, keepdims=True)
        - normed * jnp.mean(scaled * normed, axis=-1, keepdims=True)
    )
    return (spread * inner, jnp.sum(upstream * normed, axis=0), jnp.sum(upstream, axis=0))


def allowed_keys(place, pslice, prompt, length):
    shape = (pslice + length, prompt + length)
    rows = lax.broadcasted_iota(jnp.int32, shape, 0)
    cols = lax.broadcasted_iota(jnp.int32, shape, 1)
    prompt_row = rows < pslice
    prompt_col = cols < prompt
    early = prompt_row & prompt_col & (cols <= place * pslice + rows)
    later = jnp.logical_not(prompt_row) & (prompt_col | (cols - prompt <= rows - pslice))
    return early | later


def dense_weights(qkv_weight, out_weight):
    return (
        lax.all_gather(qkv_weight, "fsdp", axis=1, tiled=True),
        lax.all_gather(out_weight, "fsdp", axis=1, tiled=True),
    )


def expert_weights(up_weight, down_weight, up_shift, down_shift, centroids):
    return (
        lax.all_gather(up_weight, ("ctx", "tp"), axis=1, tiled=True),
        lax.all_gather(down_weight, ("ctx", "tp"), axis=1, tiled=True),
        lax.all_gather(up_shift, ("ctx", "tp"), axis=1, tiled=True),
        lax.all_gather(down_shift, ("ctx", "tp"), axis=1, tiled=True),
        lax.all_gather(centroids, ("ctx", "tp"), axis=1, tiled=True),
    )


def tp_rows(rows):
    return lax.all_gather(rows, "tp", axis=0, tiled=True)


def head_total(terms):
    return lax.psum(terms.astype(jnp.bfloat16), "tp").astype(jnp.float32)


def split_heads(matrix):
    return matrix.reshape(matrix.shape[0], -1, HEAD_DIM).transpose(1, 0, 2)


def join_heads(stacked):
    return stacked.transpose(1, 0, 2).reshape(stacked.shape[1], -1)


def head_forward(allowed, scale, parts):
    query, keys, values = parts
    raw = jnp.einsum("qd,kd->qk", query, keys, preferred_element_type=jnp.float32) * scale
    scores = jnp.where(allowed, raw, NEG)
    top = jnp.max(scores, axis=-1, keepdims=True)
    weights = jnp.exp(scores - top)
    total = jnp.sum(weights, axis=-1, keepdims=True)
    shares = (weights / total).astype(jnp.bfloat16)
    context = jnp.dot(shares, values, preferred_element_type=jnp.float32).astype(jnp.bfloat16)
    return (context, (top + jnp.log(total))[:, 0])


def head_backward(allowed, scale, parts):
    query, keys, values, context_grad, log_total = parts
    raw = jnp.einsum("qd,kd->qk", query, keys, preferred_element_type=jnp.float32) * scale
    scores = jnp.where(allowed, raw, NEG)
    weights = jnp.exp(scores - log_total[:, None])
    values_grad = jnp.einsum(
        "qk,qd->kd", weights.astype(jnp.bfloat16), context_grad, preferred_element_type=jnp.float32
    )
    weight_grad = jnp.einsum("qd,kd->qk", context_grad, values, preferred_element_type=jnp.float32)
    row_dot = jnp.sum(weights * weight_grad, axis=-1, keepdims=True)
    logit_grad = (weights * (weight_grad - row_dot)).astype(jnp.bfloat16)
    query_grad = jnp.dot(logit_grad, keys, preferred_element_type=jnp.float32) * scale
    keys_grad = (
        jnp.einsum("qk,qd->kd", logit_grad, query, preferred_element_type=jnp.float32) * scale
    )
    return (query_grad, keys_grad, values_grad)


def shards(
    tokens,
    cotangent,
    routes,
    qkv_weight,
    out_weight,
    layer_norm_gains,
    layer_norm_biases,
    up_weight,
    up_shift,
    down_weight,
    down_shift,
    centroids,
):
    block = tokens.shape[2]
    width = tokens.shape[3]
    pslice = block - LEN
    half = routes.shape[2]
    place = lax.axis_index("ctx")
    half_start = lax.axis_index("tp") * half
    scale = HEAD_DIM ** (-0.5)
    residual_stream = tokens.reshape(block, width).astype(jnp.float32)
    project_full, output_full = dense_weights(qkv_weight, out_weight)
    first_normed_rows, first_standardized, first_deviation = norm_input_rows(
        residual_stream, layer_norm_gains[0], layer_norm_biases[0]
    )
    first = first_normed_rows.astype(jnp.bfloat16)
    projected = jnp.einsum(
        "rd,jde->jre", first, project_full, preferred_element_type=jnp.float32
    ).astype(jnp.bfloat16)
    queries, keys_own, values_own = (projected[0], projected[1], projected[2])
    prompt_keys, prompt_values = (
        lax.all_gather(keys_own[:pslice], "ctx", axis=0, tiled=True),
        lax.all_gather(values_own[:pslice], "ctx", axis=0, tiled=True),
    )
    keys_all = jnp.concatenate([prompt_keys, keys_own[pslice:]], axis=0)
    values_all = jnp.concatenate([prompt_values, values_own[pslice:]], axis=0)
    allowed = allowed_keys(place, pslice, PROMPT, LEN)
    query_heads = split_heads(queries)
    key_heads = split_heads(keys_all)
    value_heads = split_heads(values_all)
    context_heads, log_total = lax.map(
        partial(head_forward, allowed, scale), (query_heads, key_heads, value_heads)
    )
    context = join_heads(context_heads)
    attended = head_total(jnp.dot(context, output_full, preferred_element_type=jnp.float32))
    residual_rows = residual_stream + attended
    second_normed_rows, second_standardized, second_deviation = norm_input_rows(
        residual_rows, layer_norm_gains[1], layer_norm_biases[1]
    )
    second = second_normed_rows.astype(jnp.bfloat16)
    own_rows = lax.dynamic_slice_in_dim(second, half_start, half, 0)
    route = routes.reshape(half)
    local_experts = up_weight.shape[0]
    owners = lax.axis_size("fsdp")
    total_experts = local_experts * owners
    capacity = 2 * half // total_experts
    slots = total_experts * capacity
    member = (route[:, None] == lax.broadcasted_iota(jnp.int32, (half, total_experts), 1)).astype(
        jnp.int32
    )
    rank = jnp.sum((jnp.cumsum(member, axis=0) - 1) * member, axis=1)
    slot_of = route * capacity + rank
    placing = (lax.broadcasted_iota(jnp.int32, (slots, half), 0) == slot_of[None, :]).astype(
        jnp.bfloat16
    )
    outgoing = (
        jnp.dot(placing, own_rows, preferred_element_type=jnp.float32)
        .astype(jnp.bfloat16)
        .reshape(owners, local_experts, capacity, width)
    )
    up_full, down_full, up_bias, down_bias, centres = expert_weights(
        up_weight, down_weight, up_shift, down_shift, centroids
    )
    arrived = lax.all_to_all(outgoing, "fsdp", split_axis=0, concat_axis=0, tiled=True)
    score = jnp.einsum("sekd,ed->sek", arrived, centres, preferred_element_type=jnp.float32)
    gate = jax.nn.sigmoid(score)
    inner = jnp.einsum(
        "sekd,edf->sekf", arrived, up_full, preferred_element_type=jnp.float32
    ) + up_bias[None, :, None, :].astype(jnp.float32)
    hidden = jax.nn.gelu(inner, approximate=False).astype(jnp.bfloat16)
    result = jnp.einsum(
        "sekf,efd->sekd", hidden, down_full, preferred_element_type=jnp.float32
    ) + down_bias[None, :, None, :].astype(jnp.float32)
    sent = (gate[..., None] * result).astype(jnp.bfloat16)
    returned = lax.all_to_all(sent, "fsdp", split_axis=0, concat_axis=0, tiled=True)
    returned, arrived, inner, hidden, gate, result = (
        returned,
        arrived,
        inner,
        hidden,
        gate,
        result,
    )
    back_rows = jnp.einsum(
        "sr,sd->rd", placing, returned.reshape(slots, width), preferred_element_type=jnp.float32
    ).astype(jnp.bfloat16)
    expert_out = tp_rows(back_rows)
    mixed = (residual_rows + expert_out.astype(jnp.float32)).astype(jnp.bfloat16)
    project_back, output_back = dense_weights(qkv_weight, out_weight)
    up_back, down_back, unused_up, unused_down, centre_back = expert_weights(
        up_weight, down_weight, up_shift, down_shift, centroids
    )
    upstream_rows = cotangent.reshape(block, width)
    upstream = upstream_rows.astype(jnp.float32)
    upstream_half = lax.dynamic_slice_in_dim(upstream_rows, half_start, half, 0)
    grad_out = (
        jnp.dot(placing, upstream_half, preferred_element_type=jnp.float32)
        .astype(jnp.bfloat16)
        .reshape(owners, local_experts, capacity, width)
    )
    arrived_grad = lax.all_to_all(grad_out, "fsdp", split_axis=0, concat_axis=0, tiled=True).astype(
        jnp.float32
    )
    result_grad = (gate[..., None] * arrived_grad).astype(jnp.bfloat16)
    gate_grad = jnp.sum(arrived_grad * result, axis=-1)
    score_grad = (gate_grad * gate * (1.0 - gate)).astype(jnp.bfloat16)
    hidden_grad = jnp.einsum(
        "sekd,efd->sekf", result_grad, down_back, preferred_element_type=jnp.float32
    )
    gelu_pull = jax.vjp(partial(jax.nn.gelu, approximate=False), inner)[1]
    inner_grad = gelu_pull(hidden_grad)[0].astype(jnp.bfloat16)
    rows_grad = jnp.einsum(
        "sekf,edf->sekd", inner_grad, up_back, preferred_element_type=jnp.float32
    )
    rows_grad = rows_grad + score_grad.astype(jnp.float32)[..., None] * centre_back[
        None, :, None, :
    ].astype(jnp.float32)
    sent_grad = lax.all_to_all(
        rows_grad.astype(jnp.bfloat16), "fsdp", split_axis=0, concat_axis=0, tiled=True
    )
    up_local = jnp.einsum("sekd,sekf->edf", arrived, inner_grad, preferred_element_type=jnp.float32)
    down_local = jnp.einsum(
        "sekf,sekd->efd", hidden, result_grad, preferred_element_type=jnp.float32
    )
    up_shift_local = jnp.sum(inner_grad.astype(jnp.float32), axis=(0, 2))
    down_shift_local = jnp.sum(result_grad.astype(jnp.float32), axis=(0, 2))
    centre_local = jnp.einsum(
        "sek,sekd->ed", score_grad, arrived, preferred_element_type=jnp.float32
    )
    up_grad, down_grad, up_shift_grad, down_shift_grad, centroids_grad = (
        lax.psum_scatter(
            up_local.astype(jnp.bfloat16), ("ctx", "tp"), scatter_dimension=1, tiled=True
        ).astype(jnp.float32),
        lax.psum_scatter(
            down_local.astype(jnp.bfloat16), ("ctx", "tp"), scatter_dimension=1, tiled=True
        ).astype(jnp.float32),
        lax.psum_scatter(
            up_shift_local.astype(jnp.bfloat16), ("ctx", "tp"), scatter_dimension=1, tiled=True
        ).astype(jnp.float32),
        lax.psum_scatter(
            down_shift_local.astype(jnp.bfloat16), ("ctx", "tp"), scatter_dimension=1, tiled=True
        ).astype(jnp.float32),
        lax.psum_scatter(
            centre_local.astype(jnp.bfloat16), ("ctx", "tp"), scatter_dimension=1, tiled=True
        ).astype(jnp.float32),
    )
    half_grad = jnp.einsum(
        "sr,sd->rd", placing, sent_grad.reshape(slots, width), preferred_element_type=jnp.float32
    ).astype(jnp.bfloat16)
    second_norm_gradient = tp_rows(half_grad).astype(jnp.float32)
    resid_norm_grad, gain_two_grad, shift_two_grad = norm_back(
        second_norm_gradient, second_standardized, second_deviation, layer_norm_gains[1]
    )
    resid_grad = upstream + resid_norm_grad
    attended_grad = resid_grad.astype(jnp.bfloat16)
    output_grad = jnp.einsum(
        "rh,rd->hd", context, attended_grad, preferred_element_type=jnp.float32
    )
    context_grad = jnp.einsum(
        "rd,hd->rh", attended_grad, output_back, preferred_element_type=jnp.float32
    ).astype(jnp.bfloat16)
    query_grad, keys_grad, values_grad = lax.map(
        partial(head_backward, allowed, scale),
        (query_heads, key_heads, value_heads, split_heads(context_grad), log_total),
    )
    keys_flat = join_heads(keys_grad)
    values_flat = join_heads(values_grad)
    prompt_key_grad, prompt_value_grad = (
        lax.psum_scatter(
            keys_flat[:PROMPT].astype(jnp.bfloat16), "ctx", scatter_dimension=0, tiled=True
        ).astype(jnp.float32),
        lax.psum_scatter(
            values_flat[:PROMPT].astype(jnp.bfloat16), "ctx", scatter_dimension=0, tiled=True
        ).astype(jnp.float32),
    )
    keys_total = jnp.concatenate([prompt_key_grad, keys_flat[PROMPT:]], axis=0).astype(jnp.bfloat16)
    values_total = jnp.concatenate([prompt_value_grad, values_flat[PROMPT:]], axis=0).astype(
        jnp.bfloat16
    )
    queries_total = join_heads(query_grad).astype(jnp.bfloat16)
    stacked = jnp.stack([queries_total, keys_total, values_total])
    project_grad = jnp.einsum("rd,jre->jde", first, stacked, preferred_element_type=jnp.float32)
    first_norm_gradient = head_total(
        jnp.einsum("jre,jde->rd", stacked, project_back, preferred_element_type=jnp.float32)
    )
    stream_norm_grad, gain_one_grad, shift_one_grad = norm_back(
        first_norm_gradient, first_standardized, first_deviation, layer_norm_gains[0]
    )
    tokens_grad = resid_grad + stream_norm_grad
    gains_local = jnp.stack([gain_one_grad, gain_two_grad])
    shifts_local = jnp.stack([shift_one_grad, shift_two_grad])
    qkv_grad, out_grad, gains_grad, shifts_grad = (
        lax.psum_scatter(project_grad, ("fsdp", "ctx"), scatter_dimension=1, tiled=True),
        lax.psum_scatter(output_grad, ("fsdp", "ctx"), scatter_dimension=1, tiled=True),
        lax.psum_scatter(gains_local, ("fsdp", "ctx"), scatter_dimension=1, tiled=True),
        lax.psum_scatter(shifts_local, ("fsdp", "ctx"), scatter_dimension=1, tiled=True),
    )
    return (
        mixed.reshape(1, 1, block, width),
        tokens_grad.reshape(1, 1, block, width),
        qkv_grad,
        out_grad,
        gains_grad,
        shifts_grad,
        up_grad,
        up_shift_grad,
        down_grad,
        down_shift_grad,
        centroids_grad,
    )


def solution(mesh):
    in_specs = (
        P("fsdp", "ctx", None, None),
        P("fsdp", "ctx", None, None),
        P("fsdp", "ctx", "tp", None),
        P(None, "fsdp", "tp"),
        P("tp", "fsdp"),
        P(),
        P(),
        P("fsdp", ("ctx", "tp"), None),
        P("fsdp", ("ctx", "tp")),
        P("fsdp", ("ctx", "tp"), None),
        P("fsdp", ("ctx", "tp")),
        P("fsdp", ("ctx", "tp")),
    )
    out_specs = (
        P("fsdp", "ctx", None, None),
        P("fsdp", "ctx", None, None),
        P(None, ("fsdp", "ctx"), "tp"),
        P("tp", ("fsdp", "ctx")),
        P(None, ("fsdp", "ctx")),
        P(None, ("fsdp", "ctx")),
        P("fsdp", ("ctx", "tp"), None),
        P("fsdp", ("ctx", "tp")),
        P("fsdp", ("ctx", "tp"), None),
        P("fsdp", ("ctx", "tp")),
        P("fsdp", ("ctx", "tp")),
    )
    return jax.shard_map(shards, mesh=mesh, in_specs=in_specs, out_specs=out_specs, check_vma=False)
```

profile of v0, /device:TPU:0, one launch (start us, length us, event | category | flops | bytes accessed | tf_op | source)
XLA Modules:
  0.0 1488.9 jit_solution(16068740951477841922)
XLA Ops:
  14.4 45.3 %all-gather.12.cloned.1.call-done = bf16[3,768,384]{2,1,0:T(8,128)(2,1)} async-done(((bf16[3,96,384]{2,1,0:T(8,128)(2,1)}), bf16[3,768,384]{2,1,0:T(8,128)(2,1)}) %all-gather.12.cloned.1.call-update) | async-done | bytes 1769488 | tf_op jit(solution)/shard_map/all_gather | solution.py:48
  70.2 33.8 %all_gather.41 = bf16[384,768]{0,1:T(8,128)(2,1)} all-gather(bf16[384,96]{0,1:T(8,128)(2,1)S(1)} %copy-done.25), channel_id=1, replica_groups=mesh['fsdp'=8,'ctx'=2,'tp'=2] {'fsdp'}, dimensions={1}, use_global_device_ids=true | all-gather | bytes 663552 | tf_op jit(solution)/shard_map/all_gather | solution.py:49
  111.0 11.3 all-gather.24.cloned.1.call-done
  130.0 82.4 %while.28 = (s32[]{:T(128)}, bf16[6,1280,64]{1,2,0:T(8,128)(2,1)}, f32[6,1280]{1,0:T(8,128)}, bf16[6,1280,64]{2,1,0:T(8,128)(2,1)}, bf16[6,2304,64]{2,1,0:T(8,12...) while((s32[]{:T(128)}, bf16[6,1280,64]{1,2,0:T(8,128)(2,1)}, ...), condition=%wide.region_5.6_spmd.clone, body=%wide.region_2.5_spmd.clone.sunk | while | flops 799292160 | bytes 37163152 | solution.py:150
  130.0 6.9 fusion.199
  143.7 6.9 fusion.199
  157.4 6.9 fusion.199
  171.1 6.9 fusion.199
  184.8 6.9 fusion.199
  198.5 6.9 fusion.199
  221.2 18.6 %all-reduce.5.cloned.1.call-done = bf16[1280,768]{1,0:T(8,128)(2,1)} async-done(((bf16[1280,768]{1,0:T(8,128)(2,1)}), bf16[1280,768]{1,0:T(8,128)(2,1)}) %all-reduce.5.cloned.1.call-update) | async-done | bytes 1966096 | tf_op jit(solution)/shard_map/psum | solution.py:68
  248.7 5.7 all-to-all-start
  254.4 5.4 all_gather.44
  259.8 5.2 all-gather.2
  265.1 5.2 all-gather.3
  274.0 26.3 %all-to-all-done = bf16[8,2,80,768]{3,2,1,0:T(8,128)(2,1)} async-done(((bf16[8,2,80,768]{3,2,1,0:T(8,128)(2,1)}), bf16[8,2,80,768]{3,2,1,0:T(8,128)(2,1)}, u32[]{:S(2)}, u32[]{:S(2)}) %all-to-all-start) | async-done | bytes 1966112 | tf_op jit(solution)/shard_map/all_to_all | solution.py:183
  306.4 43.9 %fusion.66 = (bf16[8,2,80,3072]{3,2,0,1:T(8,128)(2,1)}, f32[8,2,80,3072]{3,2,0,1:T(8,128)}, f32[2,8,80,3072]{3,2,1,0:T(8,128)}) fusion(f32[2,3072]{1,0:T(2,128)S(1)} %convert_element_type.197, bf16[2,768,3072]{2,1,0:T(8,128)(2,1)} %all-gather.14.cloned.1.call-done, bf16[8,2,80,768]{3,2,1,0:T(8,128)(2,1)} %all-to-all-done), kind=kOutput, calls=%fused_computation.82 | convolution fusion | flops 6299320320 | bytes 50749440 | tf_op jit(solution)/shard_map/sekd,edf->sekf/dot_general | solution.py:186
  350.3 13.3 fusion.110
  364.2 22.8 %fusion.167 = (bf16[2,3072]{1,0:T(2,128)(2,1)}, bf16[8,2,80,3072]{3,2,0,1:T(8,128)(2,1)}) fusion(f32[8,2,80,3072]{3,2,0,1:T(8,128)} %get-tuple-element.291, bf16[2,3072,768]{2,1,0:T(8,128)(2,1)} %all-gather.16.cloned.1.call-done, f32[8,2,80]{2,0,1:T(8,128)S(1)} %divide_bitcast_fusion, bf16[8,2,80,768]{3,2,1,0:T(8,128)(2,1)S(1)} %all-to-all-done.2, ...), kind=kOutput, calls=%fused_computation.234 | convolution fusion | flops 6105655296 | bytes 50766848 | tf_op jit(solution)/shard_map/sekd,efd->sekf/dot_general | solution.py:226
  387.0 11.4 fusion.118
  398.5 51.3 %all_to_all.20 = bf16[8,2,80,768]{3,2,1,0:T(8,128)(2,1)S(1)} all-to-all(bf16[8,2,80,768]{3,2,1,0:T(8,128)(2,1)S(1)} %copy.90), channel_id=1, replica_groups=mesh['fsdp'=8,'ctx'=2,'tp'=2] {'fsdp'}, dimensions={0} | all-to-all | bytes 3932160 | tf_op jit(solution)/shard_map/all_to_all | solution.py:237
  452.6 9.1 all-gather.20.cloned.1.call-done
  461.7 4.8 fusion.116
  475.4 139.7 %while.29 = (s32[]{:T(128)}, bf16[6,1280,64]{1,2,0:T(8,128)(2,1)}, bf16[6,2304,64]{1,2,0:T(8,128)(2,1)}, bf16[6,2304,64]{1,2,0:T(8,128)(2,1)}, bf16[6,1280,64]{2...) while((s32[]{:T(128)}, bf16[6,1280,64]{1,2,0:T(8,128)(2,1)}, ...), condition=%wide.region_17.18_spmd.clone, body=%wide.region_15.17_spmd.clone.sunk | while | flops 1934850816 | bytes 107280608 | solution.py:281
  479.2 8.8 multiply_reduce_fusion.3
  502.4 8.8 multiply_reduce_fusion.3
  525.5 8.8 multiply_reduce_fusion.3
  548.7 8.8 multiply_reduce_fusion.3
  571.9 8.8 multiply_reduce_fusion.3
  595.1 8.8 multiply_reduce_fusion.3
  622.9 5.8 all-to-all-start.1
  631.6 14.0 reduce-scatter.23.cloned.1.call-done
  645.7 29.0 %reduce-scatter.21.cloned.1.call-done = bf16[1024,384]{1,0:T(8,128)(2,1)} async-done(((bf16[2048,384]{1,0:T(8,128)(2,1)}), bf16[1024,384]{1,0:T(8,128)(2,1)}) %reduce-scatter.21.cloned.1.call-update) | async-done | bytes 786448 | tf_op jit(solution)/shard_map/reduce_scatter | solution.py:288
  674.7 6.1 bitcast_convert_fusion.2
  691.1 10.9 all-reduce.7.cloned.1.call-done
  707.5 5.9 convolution_bitcast_fusion
  713.4 6.2 copy.98
  719.7 13.1 bitcast_convert_fusion.1
  732.9 13.2 bitcast_convert_fusion
  747.3 4.4 fusion.148
  757.6 6.4 fusion.107
  763.9 117.0 %reduce-scatter.31.cloned.1.call-done = f32[48,2]{1,0:T(8,128)} async-done(((f32[768,2]{1,0:T(8,128)}), f32[48,2]{1,0:T(8,128)}) %reduce-scatter.31.cloned.1.call-update) | async-done | bytes 400
  882.3 125.4 %reduce-scatter.33.cloned.1.call-done = f32[48,2]{1,0:T(8,128)} async-done(((f32[768,2]{1,0:T(8,128)}), f32[48,2]{1,0:T(8,128)}) %reduce-scatter.33.cloned.1.call-update) | async-done | bytes 400
  1009.0 182.3 %all-reduce.9.cloned.1.call-done = f32[3,768,384]{2,0,1:T(4,128)} async-done(((f32[3,768,384]{2,0,1:T(4,128)}), f32[3,768,384]{2,0,1:T(4,128)}) %all-reduce.9.cloned.1.call-update) | async-done | bytes 3538960
  1193.1 77.6 %reduce-scatter.27.cloned.1.call-done = bf16[2,192,3072]{2,1,0:T(8,128)(2,1)} async-done(((bf16[2,768,3072]{2,1,0:T(8,128)(2,1)}), bf16[2,192,3072]{2,1,0:T(8,128)(2,1)}) %reduce-scatter.27.cloned.1.call-update) | async-done | bytes 2359312 | tf_op jit(solution)/shard_map/reduce_scatter | solution.py:250
  1270.7 4.4 convert_element_type.226
  1275.1 76.0 %reduce-scatter.29.cloned.1.call-done = bf16[2,768,768]{2,1,0:T(8,128)(2,1)} async-done(((bf16[2,3072,768]{2,1,0:T(8,128)(2,1)}), bf16[2,768,768]{2,1,0:T(8,128)(2,1)}) %reduce-scatter.29.cloned.1.call-update) | async-done | bytes 2359312 | tf_op jit(solution)/shard_map/reduce_scatter | solution.py:253
  1355.4 126.0 %reduce-scatter.25.cloned.1.call-done = f32[384,48]{0,1:T(8,128)} async-done(((f32[384,768]{0,1:T(8,128)}), f32[384,48]{0,1:T(8,128)}) %reduce-scatter.25.cloned.1.call-update) | async-done | bytes 73744 | tf_op jit(solution)/shard_map/reduce_scatter | solution.py:313
  (337 shorter events, 239.3 us)
Async XLA Ops:
  8.0 51.7 %copy-start = (bf16[1,1,1280,768]{3,2,1,0:T(8,128)(2,1)S(1)}, bf16[1,1,1280,768]{3,2,1,0:T(8,128)(2,1)}, u32[]{:S(2)}) copy-start(bf16[1,1,1280,768]{3,2,1,0:T(8,128)(2,1)} %param.16) | copy-start | bytes 5898244
  8.0 51.7 %all-gather.12.cloned.1.call-start = ((), (), s32[]{:S(2)}) async-start(), calls=%async_computation.14 | async-start | bytes 1990656 | tf_op jit(solution)/shard_map/all_gather | solution.py:48
  8.8 99.2 %all-gather.22.cloned.1.call-start = ((), (), s32[]{:S(2)}) async-start(), calls=%async_computation.26 | async-start | bytes 2359296 | tf_op jit(solution)/shard_map/all_gather | solution.py:141
  10.2 53.8 %copy-start.28 = (f32[768]{0:T(1024)}, f32[768]{0:T(1024)S(1)}, u32[]{:S(2)}) copy-start(f32[768]{0:T(1024)S(1)} %get-tuple-element.307) | copy-start | bytes 9220
  10.2 53.8 %copy-start.40 = (f32[768]{0:T(1024)}, f32[768]{0:T(1024)S(1)}, u32[]{:S(2)}) copy-start(f32[768]{0:T(1024)S(1)} %get-tuple-element.233) | copy-start | bytes 9220
  12.1 52.0 %copy-start.21 = (f32[1280]{0:T(1024)}, f32[1280]{0:T(1024)S(1)}, u32[]{:S(2)}) copy-start(f32[1280]{0:T(1024)S(1)} %broadcast_multiply_fusion.5) | copy-start | bytes 15364
  14.4 49.7 %copy-start.23 = (f32[1280]{0:T(1024)}, f32[1280]{0:T(1024)S(1)}, u32[]{:S(2)}) copy-start(f32[1280]{0:T(1024)S(1)} %add_rsqrt_fusion.1) | copy-start | bytes 15364
  67.0 37.0 %slice-start = ((bf16[3,1280,384]{1,2,0:T(8,128)(2,1)}), bf16[1,1280,384]{1,2,0:T(8,128)(2,1)S(1)}, s32[]{:S(2)}) async-start(bf16[3,1280,384]{1,2,0:T(8,128)(2,1)} %copy-done.11), calls=%async_computation.34 | async-start | bytes 1966080 | tf_op jit(solution)/shard_map/slice | solution.py:139
  67.1 55.3 %all-gather.24.cloned.1.call-start = ((), (), s32[]{:S(2)}) async-start(), calls=%async_computation.27 | async-start | bytes 2359296 | tf_op jit(solution)/shard_map/all_gather | solution.py:142
  67.8 172.0 %all-reduce.5.cloned.1.call-start = ((), (), s32[]{:S(2)}) async-start(), calls=%async_computation.15 | async-start | bytes 3932160 | tf_op jit(solution)/shard_map/psum | solution.py:68
  212.4 6.3 copy-start.37
  218.1 21.7 %copy-start.1 = (bf16[1,1,1280,768]{3,2,1,0:T(8,128)(2,1)S(1)}, bf16[1,1,1280,768]{3,2,1,0:T(8,128)(2,1)}, u32[]{:S(2)}) copy-start(bf16[1,1,1280,768]{3,2,1,0:T(8,128)(2,1)} %param.16) | copy-start | bytes 5898244
  218.1 88.3 %all-gather.14.cloned.1.call-start = ((), (), s32[]{:S(2)}) async-start(), calls=%async_computation.16 | async-start | bytes 11796480 | tf_op jit(solution)/shard_map/all_gather | solution.py:55
  218.7 131.6 %all-gather.16.cloned.1.call-start = ((), (), s32[]{:S(2)}) async-start(), calls=%async_computation.17 | async-start | bytes 11796480 | tf_op jit(solution)/shard_map/all_gather | solution.py:56
  221.1 49.8 %copy-start.42 = (s32[640]{0:T(1024)}, s32[640]{0:T(1024)S(1)}, u32[]{:S(2)}) copy-start(s32[640]{0:T(1024)S(1)} %multiply_add_fusion) | copy-start | bytes 7684
  248.7 11.1 copy-start.49
  248.7 16.4 %copy-start.50 = (bf16[2,192]{1,0:T(2,128)(2,1)S(1)}, bf16[2,192]{1,0:T(2,128)(2,1)}, u32[]{:S(2)}) copy-start(bf16[2,192]{1,0:T(2,128)(2,1)} %param.26) | copy-start | bytes 2308
  248.7 22.3 %copy-start.13 = (bf16[1,1,1280,768]{3,2,1,0:T(8,128)(2,1)S(1)}, bf16[1,1,1280,768]{3,2,1,0:T(8,128)(2,1)}, u32[]{:S(2)}) copy-start(bf16[1,1,1280,768]{3,2,1,0:T(8,128)(2,1)} %param.17) | copy-start | bytes 5898244
  248.7 51.6 %all-to-all-start = ((bf16[8,2,80,768]{3,2,1,0:T(8,128)(2,1)}), bf16[8,2,80,768]{3,2,1,0:T(8,128)(2,1)}, u32[]{:S(2)}, u32[]{:S(2)}) async-start(bf16[8,2,80,768]{3,2,1,0:T(8,128)(2,1)} %bitcast.381), calls=%async_computation | async-start | bytes 3932160 | tf_op jit(solution)/shard_map/all_to_all | solution.py:183
  300.3 49.9 %all-to-all-start.2 = ((bf16[8,2,80,768]{3,2,1,0:T(8,128)(2,1)}), bf16[8,2,80,768]{3,2,1,0:T(8,128)(2,1)S(1)}, u32[]{:S(2)}, u32[]{:S(2)}) async-start(bf16[8,2,80,768]{3,2,1,0:T(8,128)(2,1)} %bitcast.380), calls=%async_computation.2 | async-start | bytes 3932160 | tf_op jit(solution)/shard_map/all_to_all | solution.py:220
  303.9 157.8 %all-gather.20.cloned.1.call-start = ((), (), s32[]{:S(2)}) async-start(), calls=%async_computation.19 | async-start | bytes 2949120 | tf_op jit(solution)/shard_map/all_gather | solution.py:64
  306.3 57.9 %copy-start.32 = (f32[8,2,80]{2,0,1:T(8,128)}, f32[8,2,80]{2,0,1:T(8,128)S(1)}, u32[]{:S(2)}) copy-start(f32[8,2,80]{2,0,1:T(8,128)S(1)} %divide_bitcast_fusion) | copy-start | bytes 15364
  350.2 13.9 copy-start.9
  364.2 22.8 %copy-start.39 = (f32[2,768]{1,0:T(2,128)S(1)}, f32[2,768]{1,0:T(2,128)}, u32[]{:S(2)}) copy-start(f32[2,768]{1,0:T(2,128)} %bitcast_convert_fusion.4) | copy-start | bytes 18436
  398.4 51.4 %copy-start.43 = (s32[640]{0:T(1024)S(1)}, s32[640]{0:T(1024)}, u32[]{:S(2)}) copy-start(s32[640]{0:T(1024)} %copy-done.42) | copy-start | bytes 7684
  449.8 11.9 copy-start.31
  449.8 16.7 %copy-start.14 = (bf16[1,1,1280,768]{3,2,1,0:T(8,128)(2,1)S(1)}, bf16[1,1,1280,768]{3,2,1,0:T(8,128)(2,1)}, u32[]{:S(2)}) copy-start(bf16[1,1,1280,768]{3,2,1,0:T(8,128)(2,1)} %param.17) | copy-start | bytes 5898244
  452.5 14.0 copy-start.27
  452.5 193.2 %reduce-scatter.23.cloned.1.call-start = ((), (), s32[]{:S(2)}) async-start(), calls=%async_computation.21 | async-start | bytes 2359296 | tf_op jit(solution)/shard_map/reduce_scatter | solution.py:291
  618.2 56.5 %reduce-scatter.21.cloned.1.call-start = ((), (), s32[]{:S(2)}) async-start(), calls=%async_computation.20 | async-start | bytes 2359296 | tf_op jit(solution)/shard_map/reduce_scatter | solution.py:288
  621.5 9.5 copy-start.20
  622.9 63.6 %all-to-all-start.1 = ((bf16[8,2,80,768]{3,2,1,0:T(8,128)(2,1)}), bf16[8,2,80,768]{3,2,1,0:T(8,128)(2,1)}, u32[]{:S(2)}, u32[]{:S(2)}) async-start(bf16[8,2,80,768]{3,2,1,0:T(8,128)(2,1)} %copy.88), calls=%async_computation.1 | async-start | bytes 3932160 | tf_op jit(solution)/shard_map/all_to_all | solution.py:194
  628.7 73.3 %all-reduce.7.cloned.1.call-start = ((), (), s32[]{:S(2)}) async-start(), calls=%async_computation.22 | async-start | bytes 3932160 | tf_op jit(solution)/shard_map/psum | solution.py:68
  680.8 72.1 %reduce-scatter.37.cloned.1.call-start = ((), (), s32[]{:S(2)}) async-start(), calls=%async_computation.31 | async-start | bytes 245760
  682.2 72.2 %reduce-scatter.39.cloned.1.call-start = ((), (), s32[]{:S(2)}) async-start(), calls=%async_computation.32 | async-start | bytes 245760
  685.2 70.7 %reduce-scatter.35.cloned.1.call-start = ((), (), s32[]{:S(2)}) async-start(), calls=%async_computation.30 | async-start | bytes 983040
  686.5 71.1 %all-gather.18.cloned.1.call-start = ((), (), s32[]{:S(2)}) async-start(), calls=%async_computation.18 | async-start | bytes 2949120 | tf_op jit(solution)/shard_map/all_gather | solution.py:64
  686.6 15.4 %copy-start.2 = (bf16[1,1,1280,768]{3,2,1,0:T(8,128)(2,1)S(1)}, bf16[1,1,1280,768]{3,2,1,0:T(8,128)(2,1)}, u32[]{:S(2)}) copy-start(bf16[1,1,1280,768]{3,2,1,0:T(8,128)(2,1)} %param.16) | copy-start | bytes 5898244
  686.6 15.4 %copy-start.22 = (f32[1280]{0:T(1024)S(1)}, f32[1280]{0:T(1024)}, u32[]{:S(2)}) copy-start(f32[1280]{0:T(1024)} %copy-done.21) | copy-start | bytes 15364
  686.6 15.4 %copy-start.24 = (f32[1280]{0:T(1024)S(1)}, f32[1280]{0:T(1024)}, u32[]{:S(2)}) copy-start(f32[1280]{0:T(1024)} %copy-done.23) | copy-start | bytes 15364
  686.6 15.4 %copy-start.29 = (f32[768]{0:T(1024)S(1)}, f32[768]{0:T(1024)}, u32[]{:S(2)}) copy-start(f32[768]{0:T(1024)} %copy-done.28) | copy-start | bytes 9220
  691.0 16.5 %copy-start.41 = (f32[768]{0:T(1024)S(1)}, f32[768]{0:T(1024)}, u32[]{:S(2)}) copy-start(f32[768]{0:T(1024)} %copy-done.40) | copy-start | bytes 9220
  691.0 189.9 %reduce-scatter.31.cloned.1.call-start = ((), (), s32[]{:S(2)}) async-start(), calls=%async_computation.28 | async-start | bytes 417792
  706.4 301.3 %reduce-scatter.33.cloned.1.call-start = ((), (), s32[]{:S(2)}) async-start(), calls=%async_computation.29 | async-start | bytes 417792
  707.5 483.9 %all-reduce.9.cloned.1.call-start = ((), (), s32[]{:S(2)}) async-start(), calls=%async_computation.33 | async-start | bytes 9437184
  719.7 551.0 %reduce-scatter.27.cloned.1.call-start = ((), (), s32[]{:S(2)}) async-start(), calls=%async_computation.24 | async-start | bytes 11796480 | tf_op jit(solution)/shard_map/reduce_scatter | solution.py:250
  732.9 618.3 %reduce-scatter.29.cloned.1.call-start = ((), (), s32[]{:S(2)}) async-start(), calls=%async_computation.25 | async-start | bytes 11796480 | tf_op jit(solution)/shard_map/reduce_scatter | solution.py:253
  746.1 735.2 %reduce-scatter.25.cloned.1.call-start = ((), (), s32[]{:S(2)}) async-start(), calls=%async_computation.23 | async-start | bytes 1253376 | tf_op jit(solution)/shard_map/reduce_scatter | solution.py:313
  (38 other events, 117.4 us)
Sparse Core Ops, SparseCore 0:
  11.0 48.6 all-gather.11
  67.2 25.7 all-gather.21
  95.1 27.1 all-gather.23
  218.2 21.4 all-reduce.4
  452.6 9.0 all-gather.19
  618.3 27.3 reduce-scatter.22
  648.5 26.1 reduce-scatter.20
  680.9 21.0 all-reduce.6
  703.6 11.5 all-gather.17
Sparse Core Ops, SparseCore 1:
  220.1 64.2 all-gather.13
  285.8 64.1 all-gather.15
  684.3 19.8 reduce-scatter.36
  706.6 20.7 reduce-scatter.38
  729.9 23.1 reduce-scatter.34
  757.8 123.1 reduce-scatter.30
  885.4 122.2 reduce-scatter.32
  1013.8 177.5 all-reduce.8
  1193.8 76.8 reduce-scatter.26
  1273.3 77.8 reduce-scatter.28
  1356.4 124.9 reduce-scatter.24
where the time goes:
time: 1500 us; the launch traced here: 1490 us
  waiting for transfers between devices  872 us (58%)
  matrix products  344 us (23%)
  blocking collectives  101 us (7%)
  local copies, waits for them, and re-layouts  73.5 us (5%)
  other arithmetic  64.7 us (4%)
  between operations  17.3 us (1%)
  starting transfers between devices  15.9 us (1%)
    unnamed x26, waiting for transfers between devices  427 us
    reduce_scatter x1, waiting for transfers between devices, shards(): lax.psum_scatter(output_grad, ('fsdp', 'ctx'), scatter_dimension=1, tiled...  126 us
    reduce_scatter x1, waiting for transfers between devices, shards(): lax.psum_scatter(up_local.astype(jnp.bfloat16), ('ctx', 'tp'), scatter_di...  77.6 us
    reduce_scatter x1, waiting for transfers between devices, shards(): lax.psum_scatter(down_local.astype(jnp.bfloat16), ('ctx', 'tp'), scatter_...  76 us
    dot_general x6, matrix products, head_backward(): jnp.einsum('qd,kd->qk', query, keys, preferred_element_type=jnp.float32)  53 us
    all_to_all x1, blocking collectives, shards(): lax.all_to_all(rows_grad.astype(jnp.bfloat16), 'fsdp', split_axis=0, conc...  51.3 us
    all_gather x1, waiting for transfers between devices, dense_weights(): lax.all_gather(qkv_weight, 'fsdp', axis=1, tiled=True)  45.3 us
    dot_general x1, matrix products, shards(): jnp.einsum('sekd,edf->sekf', arrived, up_full, preferred_element_type=jnp...  43.9 us
  transfers between devices with their start and end apart: 23, of which 14 were waited for; matrix products, arithmetic and copies ran while one was open for 11% of the time, Pallas kernels for 0%

commit v1 on v0

--- a/solution.py
+++ b/solution.py
@@ -3,6 +3,8 @@
 import jax
 import jax.numpy as jnp
 from jax import lax
+from jax.experimental import pallas as pl
+from jax.experimental.pallas import tpu as pltpu
 from jax.sharding import PartitionSpec as P
 
 HEAD_DIM = 64
@@ -106,7 +108,7 @@
     return (query_grad, keys_grad, values_grad)
 
 
-def shards(
+def shards_any(
     tokens,
     cotangent,
     routes,
@@ -329,7 +331,506 @@
     )
 
 
+F32=jnp.float32; BF=jnp.bfloat16
+HD=64; NT=(((1,),(1,)),((),()))
+TILE=256
+
+def nt(a,b): return lax.dot_general(a,b,NT,preferred_element_type=F32)
+def mm(a,b): return jnp.dot(a,b,preferred_element_type=F32)
+def head_masks(rows):
+    lane=lax.broadcasted_iota(jnp.int32,(rows,2*HD),1)
+    return (lane<HD,lane>=HD)
+
+def self_forward(q_ref,k_ref,v_ref,o_ref,lse_ref):
+    rows=q_ref.shape[0]
+    lo,hi=head_masks(TILE)
+    tri=lax.broadcasted_iota(jnp.int32,(TILE,TILE),1)<=lax.broadcasted_iota(jnp.int32,(TILE,TILE),0)
+    for i in range(rows//TILE):
+        at=pl.ds(i*TILE,TILE)
+        q=q_ref[at,:]*jnp.asarray(HD**-0.5,BF)
+        outs=[];lses=[]
+        for mask in (lo,hi):
+            qm=jnp.where(mask,q,jnp.zeros_like(q))
+            diag=jnp.where(tri,nt(qm,k_ref[at,:]),-1e30)
+            top=jnp.max(diag,axis=1,keepdims=True)
+            if i:
+                off=nt(qm,k_ref[:i*TILE,:])
+                top=jnp.maximum(top,jnp.max(off,axis=1,keepdims=True))
+            pd=jnp.exp(diag-top)
+            total=jnp.sum(pd,axis=1,keepdims=True)
+            acc=mm(pd.astype(BF),v_ref[at,:])
+            if i:
+                po=jnp.exp(off-top)
+                total=total+jnp.sum(po,axis=1,keepdims=True)
+                acc=acc+mm(po.astype(BF),v_ref[:i*TILE,:])
+            outs.append(acc/total); lses.append(top+jnp.log(total))
+        o_ref[at,:]=jnp.where(lo,outs[0],outs[1])
+        lse_ref[at,:]=jnp.where(lo,lses[0],lses[1])
+
+def cross_forward(place_ref,q_ref,k_ref,v_ref,o_ref,lse_ref,ctx_ref,lse_t_ref):
+    rows=q_ref.shape[0]
+    lo,hi=head_masks(TILE)
+    def put(i,o,lse):
+        at=pl.ds(i*TILE,TILE)
+        ctx_ref[at,:]=o.astype(BF)
+        flipped=lse.T
+        lse_t_ref[0:1,at]=flipped[0:1,:]
+        lse_t_ref[1:2,at]=flipped[HD:HD+1,:]
+    def tile(i):
+        at=pl.ds(i*TILE,TILE)
+        q=q_ref[at,:]*jnp.asarray(HD**-0.5,BF)
+        outs=[];lses=[]
+        for mask in (lo,hi):
+            s=nt(jnp.where(mask,q,jnp.zeros_like(q)),k_ref[...])
+            top=jnp.max(s,axis=1,keepdims=True)
+            p=jnp.exp(s-top)
+            total=jnp.sum(p,axis=1,keepdims=True)
+            outs.append(mm(p.astype(BF),v_ref[...])/total); lses.append(top+jnp.log(total))
+        o2=jnp.where(lo,outs[0],outs[1]); l2=jnp.where(lo,lses[0],lses[1])
+        o1=o_ref[at,:]; l1=lse_ref[at,:]
+        top=jnp.maximum(l1,l2)
+        e1=jnp.exp(l1-top); e2=jnp.exp(l2-top)
+        both=e1+e2
+        put(i,(o1*e1+o2*e2)/both,top+jnp.log(both))
+    own=k_ref.shape[0]//TILE
+    later=place_ref[0]==1
+    for i in range(rows//TILE):
+        if i>=own: tile(i)
+        else:
+            pl.when(later)(partial(tile,i))
+            @pl.when(jnp.logical_not(later))
+            def _():
+                at=pl.ds(i*TILE,TILE)
+                put(i,o_ref[at,:],lse_ref[at,:])
+
+def col(rows,j=None,off=0):
+    if j is None: return pl.BlockSpec((rows,2*HD),lambda p,*_:(0,p))
+    return pl.BlockSpec((None,rows,2*HD),lambda p,*_:(j,0,p))
+
+def run_self_forward(qkv):
+    _,rows,width=qkv.shape
+    return pl.pallas_call(self_forward,grid=(width//128,),
+        in_specs=[col(rows,0),col(rows,1),col(rows,2)],
+        out_specs=[col(rows),col(rows)],
+        out_shape=[jax.ShapeDtypeStruct((rows,width),F32)]*2,name="self_forward")(qkv,qkv,qkv)
+
+def run_cross_forward(place,qkv,k,v,o,lse):
+    _,rows,width=qkv.shape; keys=k.shape[0]
+    return pl.pallas_call(cross_forward,
+        grid_spec=pltpu.PrefetchScalarGridSpec(num_scalar_prefetch=1,grid=(width//128,),
+        in_specs=[col(rows,0),col(keys),col(keys),col(rows),col(rows)],
+        out_specs=[col(rows),pl.BlockSpec((None,2,rows),lambda p,*_:(p,0,0))]),
+        out_shape=[jax.ShapeDtypeStruct((rows,width),BF),jax.ShapeDtypeStruct((width//128,2,rows),F32)],name="cross_forward")(place,qkv,k,v,o,lse)
+
+def row_dots(g,o):
+    prod=(g.astype(F32)*o.astype(F32)).T
+    return jnp.sum(prod[:HD],axis=0,keepdims=True),jnp.sum(prod[HD:],axis=0,keepdims=True)
+
+def pair_back(q,g,k,v,kt,lse,dots,masks,visible):
+    ps=[];ds=[];qs=[];gs=[];dq=[]
+    for h in range(2):
+        qm=jnp.where(masks[h],q,jnp.zeros_like(q)); gm=jnp.where(masks[h],g,jnp.zeros_like(g))
+        s=nt(k,qm)
+        p=jnp.exp(s-lse[h])
+        if visible is not None: p=jnp.where(visible,p,0.0)
+        dp=nt(v,gm)
+        d=(p*(dp-dots[h])).astype(BF)
+        ps.append(p.astype(BF)); ds.append(d); qs.append(qm); gs.append(gm)
+        dq.append(mm(kt[h*HD:(h+1)*HD,:],d))
+    dv=mm(jnp.concatenate(ps,axis=1),jnp.concatenate(gs,axis=0))
+    dk=mm(jnp.concatenate(ds,axis=1),jnp.concatenate(qs,axis=0))
+    return jnp.concatenate(dq,axis=0),dk,dv
+
+def cross_backward(place_ref,q_ref,k_ref,v_ref,g_ref,c_ref,lse_ref,dq_ref,dk_ref,dv_ref,dk_acc,dv_acc):
+    rows=q_ref.shape[0]
+    masks=head_masks(TILE)
+    keys=k_ref.shape[0]
+    dk_acc[...]=jnp.zeros_like(dk_acc); dv_acc[...]=jnp.zeros_like(dv_acc)
+    kt=k_ref[...].T
+    def tile(i):
+        at=pl.ds(i*TILE,TILE)
+        q=q_ref[at,:]*jnp.asarray(HD**-0.5,BF); g=g_ref[at,:]
+        dots=row_dots(g,c_ref[at,:])
+        lse=(lse_ref[0:1,at],lse_ref[1:2,at])
+        dq,dk,dv=pair_back(q,g,k_ref[...],v_ref[...],kt,lse,dots,masks,None)
+        dq_ref[:,at]=dq; dk_acc[...]+=dk; dv_acc[...]+=dv
+    later=place_ref[0]==1
+    for i in range(rows//TILE):
+        if i>=keys//TILE: tile(i)
+        else:
+            pl.when(later)(partial(tile,i))
+            @pl.when(jnp.logical_not(later))
+            def _(): dq_ref[:,pl.ds(i*TILE,TILE)]=jnp.zeros((2*HD,TILE),F32)
+    dk_ref[...]=dk_acc[...].astype(BF); dv_ref[...]=dv_acc[...].astype(BF)
+
+def self_backward(q_ref,k_ref,v_ref,g_ref,c_ref,lse_ref,dqx_ref,dq_ref,dk_ref,dv_ref,dk_acc,dv_acc):
+    rows=q_ref.shape[0]
+    masks=head_masks(TILE)
+    dk_acc[...]=jnp.zeros_like(dk_acc); dv_acc[...]=jnp.zeros_like(dv_acc)
+    kt=k_ref[...].T
+    seen=lax.broadcasted_iota(jnp.int32,(TILE,TILE),0)<=lax.broadcasted_iota(jnp.int32,(TILE,TILE),1)
+    for i in range(rows//TILE):
+        at=pl.ds(i*TILE,TILE)
+        q=q_ref[at,:]*jnp.asarray(HD**-0.5,BF); g=g_ref[at,:]
+        dots=row_dots(g,c_ref[at,:])
+        lse=(lse_ref[0:1,at],lse_ref[1:2,at])
+        dq,dk,dv=pair_back(q,g,k_ref[at,:],v_ref[at,:],kt[:,i*TILE:(i+1)*TILE],lse,dots,masks,seen)
+        dk_acc[at,:]+=dk; dv_acc[at,:]+=dv
+        if i:
+            n=i*TILE
+            dq2,dk,dv=pair_back(q,g,k_ref[:n,:],v_ref[:n,:],kt[:,:n],lse,dots,masks,None)
+            dq=dq+dq2
+            dk_acc[:n,:]+=dk; dv_acc[:n,:]+=dv
+        dq_ref[at,:]=((dq+dqx_ref[:,at])*(HD**-0.5)).T.astype(BF)
+    dk_ref[...]=dk_acc[...].astype(dk_ref.dtype); dv_ref[...]=dv_acc[...].astype(dv_ref.dtype)
+
+def lse_spec(rows): return pl.BlockSpec((None,2,rows),lambda p,*_:(p,0,0))
+def colt(rows): return pl.BlockSpec((2*HD,rows),lambda p,*_:(p,0))
+
+def run_cross_backward(place,qkv,k,v,g,c,lse_t):
+    _,rows,width=qkv.shape; keys=k.shape[0]
+    return pl.pallas_call(cross_backward,
+        grid_spec=pltpu.PrefetchScalarGridSpec(num_scalar_prefetch=1,grid=(width//128,),
+        in_specs=[col(rows,0),col(keys),col(keys),col(rows),col(rows),lse_spec(rows)],
+        out_specs=[colt(rows),col(keys),col(keys)],
+        scratch_shapes=[pltpu.VMEM((keys,2*HD),F32)]*2),
+        out_shape=[jax.ShapeDtypeStruct((width,rows),F32)]+[jax.ShapeDtypeStruct((keys,width),BF)]*2,name="cross_backward")(place,qkv,k,v,g,c,lse_t)
+
+def run_self_backward(qkv,g,c,lse_t,dqx):
+    _,rows,width=qkv.shape
+    return pl.pallas_call(self_backward,grid=(width//128,),
+        in_specs=[col(rows,0),col(rows,1),col(rows,2),col(rows),col(rows),lse_spec(rows),colt(rows)],
+        out_specs=[col(rows)]*3,
+        out_shape=[jax.ShapeDtypeStruct((rows,width),BF)]+[jax.ShapeDtypeStruct((rows,width),F32)]*2,
+        scratch_shapes=[pltpu.VMEM((rows,2*HD),F32)]*2,name="self_backward")(qkv,qkv,qkv,g,c,lse_t,dqx)
+
+
+def tn(a,b): return lax.dot_general(a,b,(((0,),(0,)),((),())),preferred_element_type=F32)
+RT2=0.7071067811865476; IRT2PI=0.3989422804014327
+
+def expert_step(order_ref,x_ref,cot_ref,up_ref,down_ref,ub_ref,db_ref,cen_ref,
+                sent_ref,dx_ref,gu_ref,ku_ref,gd_ref,kd_ref,us_ref,ds_ref,cg_ref,
+                rg,xt,gate,res,dx):
+    j=pl.program_id(0); last=pl.num_programs(0)-1
+    half=(last+1)//2
+    quarter=x_ref.shape[-1]//4
+    @pl.when(j==0)
+    def _():
+        x=x_ref[...]
+        score=jnp.sum(x.astype(F32)*cen_ref[...].astype(F32),axis=1,keepdims=True)
+        g=jax.nn.sigmoid(score)
+        gate[...]=jnp.broadcast_to(g,gate.shape)
+        r=(g*cot_ref[...].astype(F32)).astype(BF)
+        rg[...]=r
+        ds_ref[...]=jnp.sum(r.astype(F32),axis=0,keepdims=True)
+        t=x.T
+        for s in range(4):
+            xt[pl.ds(order_ref[4+s]*quarter,quarter),:]=t[s*quarter:(s+1)*quarter,:]
+        res[...]=jnp.zeros_like(res); dx[...]=jnp.zeros_like(dx)
+    x=x_ref[...]; r=rg[...]
+    inner=mm(x,up_ref[...])+ub_ref[...].astype(F32)
+    cdf=0.5*(1.0+lax.erf(inner*RT2))
+    hidden=(inner*cdf).astype(BF)
+    slope=cdf+inner*(jnp.exp(-0.5*inner*inner)*IRT2PI)
+    res[...]+=mm(hidden,down_ref[...])
+    back=(nt(r,down_ref[...])*slope).astype(BF)
+    us_ref[...]=jnp.sum(back.astype(F32),axis=0,keepdims=True)
+    dx[...]+=nt(back,up_ref[...])
+    du=mm(xt[...],back)
+    gu_ref[...]=du[:2*quarter].astype(BF)
+    ku_ref[...]=du[2*quarter:].astype(BF)
+    dd=tn(hidden,r).astype(BF)
+    @pl.when(j<half)
+    def _(): gd_ref[...]=dd
+    @pl.when(j>=half)
+    def _(): kd_ref[...]=dd
+    @pl.when(j==last)
+    def _():
+        g=gate[:,:1]
+        out=res[...]+db_ref[...].astype(F32)
+        sent_ref[...]=(g*out).astype(BF)
+        sg=(jnp.sum(cot_ref[...].astype(F32)*out,axis=1,keepdims=True)*g*(1.0-g)).astype(BF).astype(F32)
+        dx_ref[...]=(dx[...]+sg*cen_ref[...].astype(F32)).astype(BF)
+        cg_ref[...]=jnp.sum(sg*x_ref[...].astype(F32),axis=0,keepdims=True)
+
+def run_expert(e,order,x,cot,up,down,up_bias,down_bias,centres):
+    n,w=x.shape; ff=up.shape[2]; c=ff//4
+    whole=lambda r,k: pl.BlockSpec((r,k),lambda j,o:(0,0))
+    return pl.pallas_call(expert_step,
+      grid_spec=pltpu.PrefetchScalarGridSpec(num_scalar_prefetch=1,grid=(4,),
+        in_specs=[whole(n,w),whole(n,w),
+          pl.BlockSpec((None,w,c),lambda j,o:(e,0,o[j])),
+          pl.BlockSpec((None,c,w),lambda j,o:(e,o[j],0)),
+          pl.BlockSpec((None,1,c),lambda j,o:(e,0,o[j])),
+          pl.BlockSpec((None,1,w),lambda j,o:(e,0,0)),
+          pl.BlockSpec((None,1,w),lambda j,o:(e,0,0))],
+        out_specs=[whole(n,w),whole(n,w),
+          pl.BlockSpec((w//2,c),lambda j,o:(0,o[j])),
+          pl.BlockSpec((w//2,c),lambda j,o:(0,o[j])),
+          pl.BlockSpec((None,c,w),lambda j,o:(jnp.minimum(j,1),0,0)),
+          pl.BlockSpec((None,c,w),lambda j,o:(jnp.maximum(j,2)-2,0,0)),
+          pl.BlockSpec((1,c),lambda j,o:(0,o[j])),
+          whole(1,w),whole(1,w)],
+        scratch_shapes=[pltpu.VMEM((n,w),BF),pltpu.VMEM((w,n),BF),pltpu.VMEM((n,128),F32),pltpu.VMEM((n,w),F32),pltpu.VMEM((n,w),F32)]),
+      out_shape=[jax.ShapeDtypeStruct((n,w),BF)]*2+[jax.ShapeDtypeStruct((w//2,ff),BF)]*2+[jax.ShapeDtypeStruct((2,c,w),BF)]*2+
+        [jax.ShapeDtypeStruct((1,ff),F32),jax.ShapeDtypeStruct((1,w),F32),jax.ShapeDtypeStruct((1,w),F32)],
+      name=f"expert_{e}")(order,x,cot,up,down,up_bias,down_bias,centres)
+
+
+SWAP = ((0, 1), (1, 0))
+
+
+def swap(value, axis):
+    return lax.ppermute(value, axis, SWAP)
+
+
+def join_halves(own, side):
+    half = own.shape[0]
+    other = swap(own, "tp")
+    buffer = jnp.zeros((2 * half,) + own.shape[1:], own.dtype)
+    buffer = lax.dynamic_update_slice_in_dim(buffer, own, side * half, 0)
+    return lax.dynamic_update_slice_in_dim(buffer, other, (1 - side) * half, 0)
+
+
+def scatter_rows(matrices, place):
+    count, rows, columns = matrices.shape
+    owners = lax.axis_size("fsdp")
+    piece = rows // (2 * owners)
+    split = matrices.reshape(count, owners, 2, piece, columns)
+    give = lax.dynamic_index_in_dim(split, 1 - place, 2, keepdims=False).astype(jnp.bfloat16)
+    keep = lax.dynamic_index_in_dim(split, place, 2, keepdims=False)
+    total = (keep + swap(give, "ctx").astype(jnp.float32)).astype(jnp.bfloat16)
+    total = total.transpose(1, 0, 2, 3)
+    spread = lax.all_to_all(total, "fsdp", split_axis=0, concat_axis=0, tiled=True)
+    return jnp.sum(spread.astype(jnp.float32), axis=0)
+
+
+def quarter_sums(give, keep):
+    received = [swap(part, "tp") for part in give]
+    sends = [
+        (k[0].astype(jnp.float32) + r[0].astype(jnp.float32)).astype(jnp.bfloat16)
+        for k, r in zip(keep, received)
+    ]
+    crossed = [swap(part, "ctx") for part in sends]
+    return jnp.stack(
+        [
+            k[1].astype(jnp.float32) + r[1].astype(jnp.float32) + c.astype(jnp.float32)
+            for k, r, c in zip(keep, received, crossed)
+        ]
+    )
+
+
+def shards_pair(
+    tokens,
+    cotangent,
+    routes,
+    qkv_weight,
+    out_weight,
+    layer_norm_gains,
+    layer_norm_biases,
+    up_weight,
+    up_shift,
+    down_weight,
+    down_shift,
+    centroids,
+):
+    block = tokens.shape[2]
+    width = tokens.shape[3]
+    pslice = block - LEN
+    half = routes.shape[2]
+    experts, _, ff = up_weight.shape
+    owners = lax.axis_size("fsdp")
+    place = lax.axis_index("ctx")
+    side = lax.axis_index("tp")
+    half_start = side * half
+    bf16, f32 = jnp.bfloat16, jnp.float32
+    place_word = place.reshape(1).astype(jnp.int32)
+
+    def own_half(value):
+        return lax.dynamic_slice_in_dim(value, half_start, half, 0)
+
+    def other_half(value):
+        return lax.dynamic_slice_in_dim(value, half - half_start, half, 0)
+
+    rows_in = tokens.reshape(block, width)
+    stream = rows_in.astype(f32)
+    project_full, output_full = dense_weights(qkv_weight, out_weight)
+    first_rows, first_standard, first_spread = norm_input_rows(
+        stream, layer_norm_gains[0], layer_norm_biases[0]
+    )
+    first = first_rows.astype(bf16)
+    projected = jnp.einsum(
+        "rd,jde->jre", first, project_full, preferred_element_type=f32
+    ).astype(bf16)
+    far_keys = swap(projected[1, :pslice], "ctx")
+    far_values = swap(projected[2, :pslice], "ctx")
+    near_out, near_log = run_self_forward(projected)
+    context, log_rows = run_cross_forward(
+        place_word, projected, far_keys, far_values, near_out, near_log
+    )
+
+    route = routes.reshape(half)
+    total_experts = experts * owners
+    capacity = 2 * half // total_experts
+    slots = total_experts * capacity
+    group = slots // experts
+    member = (route[:, None] == lax.broadcasted_iota(jnp.int32, (half, total_experts), 1)).astype(
+        jnp.int32
+    )
+    rank = jnp.sum((jnp.cumsum(member, axis=0) - 1) * member, axis=1)
+    slot_of = (route % experts) * group + (route // experts) * capacity + rank
+    placing = (lax.broadcasted_iota(jnp.int32, (slots, half), 0) == slot_of[None, :]).astype(bf16)
+
+    def dispatch(rows):
+        spread = jnp.dot(placing, rows, preferred_element_type=f32).astype(bf16)
+        spread = spread.reshape(experts, owners, capacity, width)
+        return [
+            lax.all_to_all(spread[e], "fsdp", split_axis=0, concat_axis=0, tiled=True).reshape(
+                group, width
+            )
+            for e in range(experts)
+        ]
+
+    def collect(parts):
+        back = [
+            lax.all_to_all(
+                part.reshape(owners, capacity, width),
+                "fsdp",
+                split_axis=0,
+                concat_axis=0,
+                tiled=True,
+            ).reshape(group, width)
+            for part in parts
+        ]
+        return jnp.einsum(
+            "sr,sd->rd", placing, jnp.concatenate(back, axis=0), preferred_element_type=f32
+        )
+
+    upstream_half = own_half(cotangent.reshape(block, width))
+    arrived_grad = dispatch(upstream_half)
+
+    sent_half = jnp.dot(other_half(context), output_full, preferred_element_type=f32).astype(bf16)
+    kept_half = jnp.dot(own_half(context), output_full, preferred_element_type=f32)
+    resid = own_half(rows_in).astype(f32) + kept_half + swap(sent_half, "tp").astype(f32)
+    second_rows, second_standard, second_spread = norm_input_rows(
+        resid, layer_norm_gains[1], layer_norm_biases[1]
+    )
+    arrived = dispatch(second_rows.astype(bf16))
+
+    up_full = lax.all_gather(up_weight, ("ctx", "tp"), axis=1, tiled=True)
+    down_full = lax.all_gather(down_weight, ("ctx", "tp"), axis=1, tiled=True)
+    vectors = lax.all_gather(
+        jnp.concatenate([up_shift, down_shift, centroids], axis=1), ("ctx", "tp"), axis=0
+    )
+    cut = ff // 4
+    thin = width // 4
+
+    def whole_vector(start, length):
+        return (
+            vectors[:, :, start : start + length].transpose(1, 0, 2).reshape(experts, 1, 4 * length)
+        )
+
+    up_bias = whole_vector(0, cut)
+    down_bias = whole_vector(cut, thin)
+    centres = whole_vector(cut + thin, thin)
+    there, here = 1 - place, place
+    chunk_order = jnp.stack(
+        [
+            there * 2 + 1 - side,
+            here * 2 + 1 - side,
+            there * 2 + side,
+            here * 2 + side,
+        ]
+    )
+    quarter = jnp.arange(4)
+    quarter_place = (quarter % 2 == side) * 2 + (quarter // 2 == place)
+    order = jnp.concatenate([chunk_order, quarter_place]).astype(jnp.int32)
+    done = [
+        run_expert(
+            e, order, arrived[e], arrived_grad[e], up_full, down_full, up_bias, down_bias, centres
+        )
+        for e in range(experts)
+    ]
+
+    half_grad = collect([d[1] for d in done]).astype(bf16).astype(f32)
+    norm_grad, gain_two, shift_two = norm_back(
+        half_grad, second_standard, second_spread, layer_norm_gains[1]
+    )
+    attended_grad = join_halves((upstream_half.astype(f32) + norm_grad).astype(bf16), side)
+
+    expert_half = collect([d[0] for d in done])
+    mixed = join_halves((resid + expert_half).astype(bf16), side)
+
+    up_grad = quarter_sums(
+        [d[2].reshape(2, thin, ff) for d in done], [d[3].reshape(2, thin, ff) for d in done]
+    )
+    down_grad = quarter_sums([d[4] for d in done], [d[5] for d in done])
+
+    def by_quarter(k, length):
+        return jnp.stack([d[k].reshape(4, length) for d in done], axis=1)
+
+    small = jnp.concatenate([by_quarter(6, cut), by_quarter(7, thin), by_quarter(8, thin)], axis=2)
+    small = small + swap(small, "tp")
+    small = small + swap(small, "ctx")
+    small = lax.dynamic_index_in_dim(small, place * 2 + side, 0, keepdims=False)
+    up_shift_grad = small[:, :cut]
+    down_shift_grad = small[:, cut : cut + thin]
+    centroids_grad = small[:, cut + thin :]
+
+    output_grad = jnp.einsum("rd,rh->dh", attended_grad, context, preferred_element_type=f32)
+    out_grad = scatter_rows(output_grad[None], place)[0].T
+    context_grad = jnp.einsum(
+        "rd,hd->rh", attended_grad, output_full, preferred_element_type=f32
+    ).astype(bf16)
+    far_query, far_keys_grad, far_values_grad = run_cross_backward(
+        place_word, projected, far_keys, far_values, context_grad, context, log_rows
+    )
+    keys_back = swap(far_keys_grad, "ctx")
+    values_back = swap(far_values_grad, "ctx")
+    queries_total, keys_near, values_near = run_self_backward(
+        projected, context_grad, context, log_rows, far_query
+    )
+
+    def with_far(near, far):
+        return jnp.concatenate(
+            [near[:pslice] + far.astype(f32), near[pslice:]], axis=0
+        ).astype(bf16)
+
+    parts = [queries_total, with_far(keys_near, keys_back), with_far(values_near, values_back)]
+    project_grad = jnp.stack(
+        [jnp.einsum("rd,re->de", first, part, preferred_element_type=f32) for part in parts]
+    )
+    qkv_grad = scatter_rows(project_grad, place)
+    first_part = sum(
+        jnp.einsum("re,de->rd", part, project_full[j], preferred_element_type=f32)
+        for j, part in enumerate(parts)
+    ).astype(bf16)
+    first_grad = first_part.astype(f32) + swap(first_part, "tp").astype(f32)
+    stream_grad, gain_one, shift_one = norm_back(
+        first_grad, first_standard, first_spread, layer_norm_gains[0]
+    )
+    tokens_grad = attended_grad.astype(f32) + stream_grad
+    two = jnp.stack([gain_two, shift_two])
+    two = two + swap(two, "tp")
+    norms = jnp.stack([gain_one, two[0], shift_one, two[1]])
+    norms = lax.psum_scatter(norms, ("fsdp", "ctx"), scatter_dimension=1, tiled=True)
+    return (
+        mixed.reshape(1, 1, block, width),
+        tokens_grad.reshape(1, 1, block, width),
+        qkv_grad,
+        out_grad,
+        norms[:2],
+        norms[2:],
+        up_grad,
+        up_shift_grad,
+        down_grad,
+        down_shift_grad,
+        centroids_grad,
+    )
+
+
 def solution(mesh):
+    paired = mesh.shape["ctx"] == 2 and mesh.shape["tp"] == 2
     in_specs = (
         P("fsdp", "ctx", None, None),
         P("fsdp", "ctx", None, None),
@@ -357,4 +858,5 @@
         P("fsdp", ("ctx", "tp")),
         P("fsdp", ("ctx", "tp")),
     )
-    return jax.shard_map(shards, mesh=mesh, in_specs=in_specs, out_specs=out_specs, check_vma=False)
+    return jax.shard_map(
+        shards_pair if paired else shards_any, mesh=mesh, in_specs=in_specs, out_specs=out_specs, check_vma=False)

time: 1500 us -> 736 us (0.49)
  waiting for transfers between devices: 872 us -> 244 us
  matrix products: 344 us -> 38.8 us
  Pallas kernels: 0 us -> 113 us
  starting transfers between devices: 15.9 us -> 75.1 us
  local copies, waits for them, and re-layouts: 73.5 us -> 51.6 us
  blocking collectives: 101 us -> 121 us
    unnamed x26 -> x5, waiting for transfers between devices: 427 us -> 104 us
    reduce_scatter x5 -> x0, waiting for transfers between devices: 323 us -> none  [the longest x1 126 us: shards(): lax.psum_scatter(output_grad, ('fsdp', 'ctx'), scatter_dimension=1, tiled...]
    dot_general x60 -> x15, matrix products: 344 us -> 38.8 us  [the longest x2 9.34 us: collect(): jnp.einsum('sr,sd->rd', placing, jnp.concatenate(back, axis=0), preferred...]
    pallas_call x0 -> x6, Pallas kernels: none -> 113 us  [the longest x2 58.3 us: run_expert(): pl.pallas_call(expert_step, grid_spec=pltpu.PrefetchScalarGridSpec(num_sc...]
    ppermute x0 -> x21, waiting for transfers between devices: none -> 66.9 us  [swap(): return lax.ppermute(value, axis, SWAP)]
    ppermute x0 -> x21, starting transfers between devices: none -> 34.8 us  [swap(): return lax.ppermute(value, axis, SWAP)]
    psum x2 -> x0, waiting for transfers between devices: 29.5 us -> none  [head_total(): return lax.psum(terms.astype(jnp.bfloat16), 'tp').astype(jnp.float32)]
    another operation x6 -> x16, other arithmetic: 1.48 us -> 27 us  [the longest x6 18.7 us: quarter_sums(): jnp.stack([k[1].astype(jnp.float32) + r[1].astype(jnp.float32) + c.astype...]
  transfers between devices with their start and end apart: 23 -> 33, of which waited for: 14 -> 9; matrix products, arithmetic and copies ran while one was open for 11% -> 20% of each run, Pallas kernels for 0% -> 16%
where the time goes in v1:
time: 736 us; the launch traced here: 729 us
  waiting for transfers between devices  244 us (33%)
  blocking collectives  121 us (16%)
  Pallas kernels  113 us (15%)
  starting transfers between devices  75.1 us (10%)
  other arithmetic  70 us (10%)
  local copies, waits for them, and re-layouts  51.6 us (7%)
  matrix products  38.8 us (5%)
  between operations  14.9 us (2%)
    unnamed x5, waiting for transfers between devices  104 us
    ppermute x21, waiting for transfers between devices, swap(): return lax.ppermute(value, axis, SWAP)  66.9 us
    pallas_call x2, Pallas kernels, run_expert(): pl.pallas_call(expert_step, grid_spec=pltpu.PrefetchScalarGridSpec(num_sc...  58.3 us
    all_gather x1, blocking collectives, dense_weights(): lax.all_gather(out_weight, 'fsdp', axis=1, tiled=True)  44.7 us
    all_gather x1, waiting for transfers between devices, dense_weights(): lax.all_gather(qkv_weight, 'fsdp', axis=1, tiled=True)  42.3 us
    ppermute x21, starting transfers between devices, swap(): return lax.ppermute(value, axis, SWAP)  34.8 us
    all_to_all x1, blocking collectives, collect(): lax.all_to_all(part.reshape(owners, capacity, width), 'fsdp', split_axis=...  30.5 us
    all_to_all x1, blocking collectives, dispatch(): lax.all_to_all(spread[e], 'fsdp', split_axis=0, concat_axis=0, tiled=True)  28.7 us
  transfers between devices with their start and end apart: 33, of which 9 were waited for; matrix products, arithmetic and copies ran while one was open for 20% of the time, Pallas kernels for 16%

profile of v1, /device:TPU:0, one launch (start us, length us, event | category | flops | bytes accessed | tf_op | source)
XLA Modules:
  0.0 729.1 jit_solution(1968029148406603065)
XLA Ops:
  13.5 3.0 convolution_convert_fusion.1
  16.5 42.3 %all-gather.6.cloned.1.call-done = bf16[3,768,384]{2,1,0:T(8,128)(2,1)} async-done(((bf16[3,96,384]{2,1,0:T(8,128)(2,1)}), bf16[3,768,384]{2,1,0:T(8,128)(2,1)}) %all-gather.6.cloned.1.call-update) | async-done | bytes 1769488 | tf_op jit(solution)/shard_map/all_gather | solution.py:50
  58.8 4.9 fusion.18.q_ref.k_ref.v_ref
  68.5 4.4 all-to-all-start.1
  72.9 44.7 %all_gather.19 = bf16[384,768]{0,1:T(8,128)(2,1)S(1)} all-gather(bf16[384,96]{0,1:T(8,128)(2,1)S(1)} %copy-done.32), channel_id=1, replica_groups=mesh['fsdp'=8,'ctx'=2,'tp'=2] {'fsdp'}, dimensions={1}, use_global_device_ids=true | all-gather | bytes 663552 | tf_op jit(solution)/shard_map/all_gather | solution.py:51
  117.6 15.7 %self_forward.1 = (f32[1280,384]{1,0:T(8,128)}, f32[1280,384]{1,0:T(8,128)}) custom-call(bf16[3,1280,384]{2,1,0:T(8,128)(2,1)} %copy-done, bf16[3,1280,384]{2,1,0:T(8,128)(2,1)} %copy-done, bf16[3,1280,384]{2,1,0:T(8,128)(2,1)} %copy-done), custom_call_target="tpu_custom_call" | custom-call | tf_op jit(solution)/shard_map/self_forward/pallas_call | solution.py:412
  134.2 6.9 cross_forward.1
  141.1 2.8 convolution_convert_fusion.4
  143.9 4.4 all-to-all-start.4
  151.1 2.1 convolution_convert_fusion.2
  154.6 19.0 %all-to-all-done.4 = bf16[8,80,768]{2,1,0:T(8,128)(2,1)} async-done(((bf16[8,80,768]{2,1,0:T(8,128)(2,1)}), bf16[8,80,768]{2,1,0:T(8,128)(2,1)}, u32[]{:S(2)}, u32[]{:S(2)}) %all-to-all-start.4) | async-done | bytes 983072 | tf_op jit(solution)/shard_map/all_to_all | solution.py:688
  173.6 28.7 %all_to_all.50 = bf16[8,80,768]{2,1,0:T(8,128)(2,1)} all-to-all(bf16[8,80,768]{2,1,0:T(8,128)(2,1)} %bitcast.228), channel_id=1, replica_groups=mesh['fsdp'=8,'ctx'=2,'tp'=2] {'fsdp'}, dimensions={0} | all-to-all | bytes 1966080 | tf_op jit(solution)/shard_map/all_to_all | solution.py:688
  202.3 4.3 all-to-all-start.3
  208.0 17.1 %all-gather.1 = bf16[4,2,1152]{2,1,0:T(2,128)(2,1)S(1)} all-gather(bf16[1,2,1152]{2,1,0:T(2,128)(2,1)} %bitcast.246), channel_id=2, replica_groups=mesh['fsdp'=8,'ctx'=2,'tp'=2] {'ctx','tp'}, dimensions={0}, use_global_device_ids=true | all-gather | bytes 23040 | tf_op jit(solution)/shard_map/all_gather | solution.py:722
  234.1 29.1 %expert_0.1 = (bf16[640,768]{1,0:T(8,128)(2,1)}, bf16[640,768]{1,0:T(8,128)(2,1)}, bf16[384,3072]{1,0:T(8,128)(2,1)}, bf16[384,3072]{1,0:T(8,128)(2,1)}, bf16[2,...) custom-call(s32[8]{0:T(128)} %concatenate.24.order_ref, ...), custom_call_target="tpu_custom_call" | custom-call | tf_op jit(solution)/shard_map/expert_0/pallas_call | solution.py:559
  263.3 6.2 all-to-all-start.6
  269.4 29.1 %expert_1.1 = (bf16[640,768]{1,0:T(8,128)(2,1)}, bf16[640,768]{1,0:T(8,128)(2,1)}, bf16[384,3072]{1,0:T(8,128)(2,1)}, bf16[384,3072]{1,0:T(8,128)(2,1)}, bf16[2,...) custom-call(s32[8]{0:T(128)} %concatenate.24.order_ref, ...), custom_call_target="tpu_custom_call" | custom-call | tf_op jit(solution)/shard_map/expert_1/pallas_call | solution.py:559
  298.6 30.5 %all_to_all.51 = bf16[8,80,768]{2,1,0:T(8,128)(2,1)} all-to-all(bf16[8,80,768]{2,1,0:T(8,128)(2,1)} %bitcast.237), channel_id=1, replica_groups=mesh['fsdp'=8,'ctx'=2,'tp'=2] {'fsdp'}, dimensions={0} | all-to-all | bytes 1966080 | tf_op jit(solution)/shard_map/all_to_all | solution.py:696
  329.1 4.2 all-to-all-start.2
  345.2 11.8 %all-to-all-done.2 = bf16[8,80,768]{2,1,0:T(8,128)(2,1)} async-done(((bf16[8,80,768]{2,1,0:T(8,128)(2,1)}), bf16[8,80,768]{2,1,0:T(8,128)(2,1)}, u32[]{:S(2)}, u32[]{:S(2)}) %all-to-all-start.2) | async-done | bytes 983072 | tf_op jit(solution)/shard_map/all_to_all | solution.py:696
  357.0 4.5 all-to-all-start.5
  381.8 5.1 fusion.39
  390.8 4.3 bitcast_dynamic-update-slice_fusion.1
  400.5 2.6 fusion.58
  405.1 2.7 fusion.59
  408.0 2.7 fusion.29
  410.8 2.2 fusion.108
  413.0 2.1 convolution_convert_fusion.3.g_ref
  415.2 8.1 %cross_backward.1 = (f32[384,1280]{1,0:T(8,128)}, bf16[1024,384]{1,0:T(8,128)(2,1)}, bf16[1024,384]{1,0:T(8,128)(2,1)}) custom-call(s32[1]{0:T(128)} %bitcast.1.place_ref, bf16[3,1280,384]{2,1,0:T(8,128)(2,1)} %copy-done, bf16[1024,384]{1,0:T(8,128)(2,1)} %copy-done.10, bf16[1024,384]{1,0:T(8,128)(2,1)} %collective-permute-done.1.v_ref, ...), custom_call_target="tpu_custom_call" | custom-call | tf_op jit(solution)/shard_map/cross_backward/pallas_call | solution.py:492
  423.3 21.0 %collective-permute-start.5 = (bf16[1024,384]{1,0:T(8,128)(2,1)}, bf16[1024,384]{1,0:T(8,128)(2,1)S(1)}, u32[]{:S(2)}, u32[]{:S(2)}) collective-permute-start(bf16[1024,384]{1,0:T(8,128)(2,1)} %get-tuple-element.50), channel_id=1, source_target_pairs={{0,2},{2,0},{1,3},{3,1},{4,6},{6,4},{5,7},{7,5},{8,10},{10,8},{9,1... | collective-permute-start | bytes 2359304 | tf_op jit(solution)/shard_map/ppermute | solution.py:584
  445.5 3.1 fusion.26
  448.5 24.2 %self_backward.1 = (bf16[1280,384]{1,0:T(8,128)(2,1)}, f32[1280,384]{1,0:T(8,128)}, f32[1280,384]{1,0:T(8,128)}) custom-call(bf16[3,1280,384]{2,1,0:T(8,128)(2,1)} %copy-done, bf16[3,1280,384]{2,1,0:T(8,128)(2,1)} %copy-done, bf16[3,1280,384]{2,1,0:T(8,128)(2,1)} %copy-done, bf16[1280,384]{1,0:T(8,128)(2,1)} %convolution_convert_fusion.3.g_ref, ...), custom_call_target="tpu_custom_call" | custom-call | tf_op jit(solution)/shard_map/self_backward/pallas_call | solution.py:501
  477.6 2.2 bitcast_dynamic-update-slice_fusion
  483.4 6.0 all-to-all-start.9
  494.9 52.8 %collective-permute-done.6 = bf16[1024,384]{1,0:T(8,128)(2,1)S(1)} collective-permute-done((bf16[1024,384]{1,0:T(8,128)(2,1)}, bf16[1024,384]{1,0:T(8,128)(2,1)S(1)}, u32[]{:S(2)}, u32[]{:S(2)}) %collective-permute-start.6) | collective-permute-done | bytes 786464 | tf_op jit(solution)/shard_map/ppermute | solution.py:584
  548.0 2.6 fusion.19
  552.2 3.9 fusion.33
  556.2 3.8 fusion.31
  560.0 3.6 fusion.28
  563.6 5.7 fusion.14
  569.3 4.0 copy.48
  573.2 2.9 convolution_bitcast_fusion.1
  584.5 2.7 pad_maximum_fusion.1
  588.6 2.7 pad_maximum_fusion
  592.4 10.6 %collective-permute-done.8 = bf16[3,8,48,384]{3,2,1,0:T(8,128)(2,1)} collective-permute-done((bf16[3,8,48,384]{3,2,1,0:T(8,128)(2,1)S(1)}, bf16[3,8,48,384]{3,2,1,0:T(8,128)(2,1)}, u32[]{:S(2)}, u32[]{:S(2)}) %collective-permute-start.8) | collective-permute-done | bytes 884768 | tf_op jit(solution)/shard_map/ppermute | solution.py:584
  605.9 6.1 all-to-all-start.8
  612.0 5.0 fusion.13
  617.0 102.4 %reduce-scatter.4.cloned.1.call-done = f32[48,4]{1,0:T(8,128)} async-done(((f32[768,4]{1,0:T(8,128)}), f32[48,4]{1,0:T(8,128)}) %reduce-scatter.4.cloned.1.call-update) | async-done | bytes 784
  (269 shorter events, 103.6 us)
Async XLA Ops:
  7.2 51.7 %all-gather.6.cloned.1.call-start = ((), (), s32[]{:S(2)}) async-start(), calls=%async_computation.11 | async-start | bytes 1990656 | tf_op jit(solution)/shard_map/all_gather | solution.py:50
  8.0 226.2 %all-gather.10.cloned.1.call-start = ((), (), s32[]{:S(2)}) async-start(), calls=%async_computation.13 | async-start | bytes 11796480 | tf_op jit(solution)/shard_map/all_gather | solution.py:721
  8.7 225.4 %all-gather.8.cloned.1.call-start = ((), (), s32[]{:S(2)}) async-start(), calls=%async_computation.12 | async-start | bytes 11796480 | tf_op jit(solution)/shard_map/all_gather | solution.py:720
  11.8 47.0 %copy-start.33 = (f32[768]{0:T(1024)}, f32[768]{0:T(1024)S(1)}, u32[]{:S(2)}) copy-start(f32[768]{0:T(1024)S(1)} %get-tuple-element.101) | copy-start | bytes 9220
  11.8 47.0 %copy-start.44 = (f32[768]{0:T(1024)}, f32[768]{0:T(1024)S(1)}, u32[]{:S(2)}) copy-start(f32[768]{0:T(1024)S(1)} %get-tuple-element.78) | copy-start | bytes 9220
  63.7 4.7 copy-start
  65.0 68.2 %collective-permute-start = (bf16[1024,384]{1,0:T(8,128)(2,1)}, bf16[1024,384]{1,0:T(8,128)(2,1)S(1)}, u32[]{:S(2)}, u32[]{:S(2)}) collective-permute-start(bf16[1024,384]{1,0:T(8,128)(2,1)} %get-tuple-element.82), channel_id=1, source_target_pairs={{0,2},{2,0},{1,3},{3,1},{4,6},{6,4},{5,7},{7,5},{8,10},{10,8},{9,1... | collective-permute-start | bytes 2359304 | tf_op jit(solution)/shard_map/ppermute | solution.py:584
  66.5 66.8 %collective-permute-start.1 = (bf16[1024,384]{1,0:T(8,128)(2,1)}, bf16[1024,384]{1,0:T(8,128)(2,1)}, u32[]{:S(2)}, u32[]{:S(2)}) collective-permute-start(bf16[1024,384]{1,0:T(8,128)(2,1)} %get-tuple-element.81), channel_id=1, source_target_pairs={{0,2},{2,0},{1,3},{3,1},{4,6},{6,4},{5,7},{7,5},{8,10},{10,8},{9,1... | collective-permute-start | bytes 2359304 | tf_op jit(solution)/shard_map/ppermute | solution.py:584
  68.5 4.4 copy-start.32
  68.5 75.4 %all-to-all-start.1 = ((bf16[8,80,768]{2,1,0:T(8,128)(2,1)}), bf16[8,80,768]{2,1,0:T(8,128)(2,1)}, u32[]{:S(2)}, u32[]{:S(2)}) async-start(bf16[8,80,768]{2,1,0:T(8,128)(2,1)} %bitcast.15), calls=%async_computation.1 | async-start | bytes 1966080 | tf_op jit(solution)/shard_map/all_to_all | solution.py:688
  141.1 7.2 copy-start.8
  143.9 4.4 collective-permute-start.2
  143.9 29.7 %all-to-all-start.4 = ((bf16[8,80,768]{2,1,0:T(8,128)(2,1)}), bf16[8,80,768]{2,1,0:T(8,128)(2,1)}, u32[]{:S(2)}, u32[]{:S(2)}) async-start(bf16[8,80,768]{2,1,0:T(8,128)(2,1)} %bitcast.226), calls=%async_computation.4 | async-start | bytes 1966080 | tf_op jit(solution)/shard_map/all_to_all | solution.py:688
  202.3 60.9 %all-to-all-start.3 = ((bf16[8,80,768]{2,1,0:T(8,128)(2,1)}), bf16[8,80,768]{2,1,0:T(8,128)(2,1)}, u32[]{:S(2)}, u32[]{:S(2)}) async-start(bf16[8,80,768]{2,1,0:T(8,128)(2,1)} %bitcast.227), calls=%async_computation.3 | async-start | bytes 1966080 | tf_op jit(solution)/shard_map/all_to_all | solution.py:688
  263.3 35.3 %all-to-all-start.6 = ((bf16[8,80,768]{2,1,0:T(8,128)(2,1)}), bf16[8,80,768]{2,1,0:T(8,128)(2,1)}, u32[]{:S(2)}, u32[]{:S(2)}) async-start(bf16[8,80,768]{2,1,0:T(8,128)(2,1)} %bitcast.236), calls=%async_computation.6 | async-start | bytes 1966080 | tf_op jit(solution)/shard_map/all_to_all | solution.py:696
  329.1 27.9 %all-to-all-start.2 = ((bf16[8,80,768]{2,1,0:T(8,128)(2,1)}), bf16[8,80,768]{2,1,0:T(8,128)(2,1)}, u32[]{:S(2)}, u32[]{:S(2)}) async-start(bf16[8,80,768]{2,1,0:T(8,128)(2,1)} %bitcast.235), calls=%async_computation.2 | async-start | bytes 1966080 | tf_op jit(solution)/shard_map/all_to_all | solution.py:696
  357.0 32.3 %all-to-all-start.5 = ((bf16[8,80,768]{2,1,0:T(8,128)(2,1)}), bf16[8,80,768]{2,1,0:T(8,128)(2,1)}, u32[]{:S(2)}, u32[]{:S(2)}) async-start(bf16[8,80,768]{2,1,0:T(8,128)(2,1)} %bitcast.233), calls=%async_computation.5 | async-start | bytes 1966080 | tf_op jit(solution)/shard_map/all_to_all | solution.py:696
  372.7 1.4 collective-permute-start.15
  375.5 4.3 collective-permute-start.16
  377.5 23.0 %collective-permute-start.17 = (bf16[2,768,768]{2,1,0:T(8,128)(2,1)}, bf16[2,768,768]{2,1,0:T(8,128)(2,1)}, u32[]{:S(2)}, u32[]{:S(2)}) collective-permute-start(bf16[2,768,768]{2,1,0:T(8,128)(2,1)} %get-tuple-element.64), channel_id=1, source_target_pairs={{0,1},{1,0},{2,3},{3,2},{4,5},{5,4},{6,7},{7,6},{8,9},{9,8},{10,11... | collective-permute-start | bytes 7077896 | tf_op jit(solution)/shard_map/ppermute | solution.py:584
  377.5 25.7 %collective-permute-start.19 = (bf16[2,768,768]{2,1,0:T(8,128)(2,1)}, bf16[2,768,768]{2,1,0:T(8,128)(2,1)}, u32[]{:S(2)}, u32[]{:S(2)}) collective-permute-start(bf16[2,768,768]{2,1,0:T(8,128)(2,1)} %get-tuple-element.66), channel_id=1, source_target_pairs={{0,1},{1,0},{2,3},{3,2},{4,5},{5,4},{6,7},{7,6},{8,9},{9,8},{10,11... | collective-permute-start | bytes 7077896 | tf_op jit(solution)/shard_map/ppermute | solution.py:584
  378.0 29.8 %collective-permute-start.11 = (bf16[2,192,3072]{2,1,0:T(8,128)(2,1)}, bf16[2,192,3072]{2,1,0:T(8,128)(2,1)}, u32[]{:S(2)}, u32[]{:S(2)}) collective-permute-start(bf16[2,192,3072]{2,1,0:T(8,128)(2,1)} %bitcast.249), channel_id=1, source_target_pairs={{0,1},{1,0},{2,3},{3,2},{4,5},{5,4},{6,7},{7,6},{8,9},{9,8},{10,11... | collective-permute-start | bytes 7077896 | tf_op jit(solution)/shard_map/ppermute | solution.py:584
  378.0 67.4 %collective-permute-start.13 = (bf16[2,192,3072]{2,1,0:T(8,128)(2,1)}, bf16[2,192,3072]{2,1,0:T(8,128)(2,1)}, u32[]{:S(2)}, u32[]{:S(2)}) collective-permute-start(bf16[2,192,3072]{2,1,0:T(8,128)(2,1)} %bitcast.248), channel_id=1, source_target_pairs={{0,1},{1,0},{2,3},{3,2},{4,5},{5,4},{6,7},{7,6},{8,9},{9,8},{10,11... | collective-permute-start | bytes 7077896 | tf_op jit(solution)/shard_map/ppermute | solution.py:584
  388.1 10.3 %collective-permute-start.10 = (f32[2,768]{1,0:T(2,128)}, f32[2,768]{1,0:T(2,128)}, u32[]{:S(2)}, u32[]{:S(2)}) collective-permute-start(f32[2,768]{1,0:T(2,128)} %pad_maximum_fusion.13), channel_id=1, source_target_pairs={{0,1},{1,0},{2,3},{3,2},{4,5},{5,4},{6,7},{7,6},{8,9},{9,8},{10,11... | collective-permute-start | bytes 18440 | tf_op jit(solution)/shard_map/ppermute | solution.py:584
  390.8 5.7 copy-start.31
  398.4 6.7 copy-start.11
  398.4 12.3 %collective-permute-start.4 = (bf16[640,768]{1,0:T(8,128)(2,1)S(1)}, bf16[640,768]{1,0:T(8,128)(2,1)S(1)}, u32[]{:S(2)}, u32[]{:S(2)}) collective-permute-start(bf16[640,768]{1,0:T(8,128)(2,1)S(1)} %get-tuple-element.80), channel_id=1, source_target_pairs={{0,1},{1,0},{2,3},{3,2},{4,5},{5,4},{6,7},{7,6},{8,9},{9,8},{10,11... | collective-permute-start | bytes 2949128 | tf_op jit(solution)/shard_map/ppermute | solution.py:584
  400.4 75.2 %collective-permute-start.3 = (bf16[640,768]{1,0:T(8,128)(2,1)}, bf16[640,768]{1,0:T(8,128)(2,1)}, u32[]{:S(2)}, u32[]{:S(2)}) collective-permute-start(bf16[640,768]{1,0:T(8,128)(2,1)} %get-tuple-element.99), channel_id=1, source_target_pairs={{0,1},{1,0},{2,3},{3,2},{4,5},{5,4},{6,7},{7,6},{8,9},{9,8},{10,11... | collective-permute-start | bytes 2949128 | tf_op jit(solution)/shard_map/ppermute | solution.py:584
  403.1 4.9 copy-start.13
  403.1 149.1 %collective-permute-start.18 = (bf16[768,768]{1,0:T(8,128)(2,1)}, bf16[768,768]{1,0:T(8,128)(2,1)}, u32[]{:S(2)}, u32[]{:S(2)}) collective-permute-start(bf16[768,768]{1,0:T(8,128)(2,1)} %fusion.58), channel_id=1, source_target_pairs={{0,2},{2,0},{1,3},{3,1},{4,6},{6,4},{5,7},{7,5},{8,10},{10,8},{9,1... | collective-permute-start | bytes 3538952 | tf_op jit(solution)/shard_map/ppermute | solution.py:584
  407.8 174.7 %collective-permute-start.20 = (bf16[768,768]{1,0:T(8,128)(2,1)}, bf16[768,768]{1,0:T(8,128)(2,1)}, u32[]{:S(2)}, u32[]{:S(2)}) collective-permute-start(bf16[768,768]{1,0:T(8,128)(2,1)} %fusion.59), channel_id=1, source_target_pairs={{0,2},{2,0},{1,3},{3,1},{4,6},{6,4},{5,7},{7,5},{8,10},{10,8},{9,1... | collective-permute-start | bytes 3538952 | tf_op jit(solution)/shard_map/ppermute | solution.py:584
  423.3 66.4 %collective-permute-start.5 = (bf16[1024,384]{1,0:T(8,128)(2,1)}, bf16[1024,384]{1,0:T(8,128)(2,1)S(1)}, u32[]{:S(2)}, u32[]{:S(2)}) collective-permute-start(bf16[1024,384]{1,0:T(8,128)(2,1)} %get-tuple-element.50), channel_id=1, source_target_pairs={{0,2},{2,0},{1,3},{3,1},{4,6},{6,4},{5,7},{7,5},{8,10},{10,8},{9,1... | collective-permute-start | bytes 2359304 | tf_op jit(solution)/shard_map/ppermute | solution.py:584
  445.4 35.2 %collective-permute-start.9 = (bf16[1,8,48,384]{3,2,1,0:T(8,128)(2,1)S(1)}, bf16[1,8,48,384]{3,2,1,0:T(8,128)(2,1)S(1)}, u32[]{:S(2)}, u32[]{:S(2)}) collective-permute-start(bf16[1,8,48,384]{3,2,1,0:T(8,128)(2,1)S(1)} %fusion.76), channel_id=1, source_target_pairs={{0,2},{2,0},{1,3},{3,1},{4,6},{6,4},{5,7},{7,5},{8,10},{10,8},{9,1... | collective-permute-start | bytes 884744 | tf_op jit(solution)/shard_map/ppermute | solution.py:584
  472.7 9.9 %copy-start.29 = (f32[768,384]{1,0:T(8,128)S(1)}, f32[768,384]{1,0:T(8,128)}, u32[]{:S(2)}) copy-start(f32[768,384]{1,0:T(8,128)} %fusion.108) | copy-start | bytes 3538948
  473.8 18.6 %copy-start.25 = (bf16[256,384]{1,0:T(8,128)(2,1)}, bf16[256,384]{1,0:T(8,128)(2,1)S(1)}, u32[]{:S(2)}) copy-start(bf16[256,384]{1,0:T(8,128)(2,1)S(1)} %slice.266) | copy-start | bytes 589828
  475.6 80.6 %collective-permute-start.12 = (bf16[192,3072]{1,0:T(8,128)(2,1)}, bf16[192,3072]{1,0:T(8,128)(2,1)}, u32[]{:S(2)}, u32[]{:S(2)}) collective-permute-start(bf16[192,3072]{1,0:T(8,128)(2,1)} %fusion.29), channel_id=1, source_target_pairs={{0,2},{2,0},{1,3},{3,1},{4,6},{6,4},{5,7},{7,5},{8,10},{10,8},{9,1... | collective-permute-start | bytes 3538952 | tf_op jit(solution)/shard_map/ppermute | solution.py:584
  480.6 79.3 %collective-permute-start.14 = (bf16[192,3072]{1,0:T(8,128)(2,1)}, bf16[192,3072]{1,0:T(8,128)(2,1)}, u32[]{:S(2)}, u32[]{:S(2)}) collective-permute-start(bf16[192,3072]{1,0:T(8,128)(2,1)} %fusion.26), channel_id=1, source_target_pairs={{0,2},{2,0},{1,3},{3,1},{4,6},{6,4},{5,7},{7,5},{8,10},{10,8},{9,1... | collective-permute-start | bytes 3538952 | tf_op jit(solution)/shard_map/ppermute | solution.py:584
  483.4 67.2 %all-to-all-start.9 = ((bf16[8,1,48,384]{3,2,1,0:T(8,128)(2,1)}), bf16[8,1,48,384]{3,2,1,0:T(8,128)(2,1)}, u32[]{:S(2)}, u32[]{:S(2)}) async-start(bf16[8,1,48,384]{3,2,1,0:T(8,128)(2,1)} %fusion.75), calls=%async_computation.9 | async-start | bytes 589824 | tf_op jit(solution)/shard_map/all_to_all | solution.py:604
  489.3 230.0 %reduce-scatter.4.cloned.1.call-start = ((), (), s32[]{:S(2)}) async-start(), calls=%async_computation.14 | async-start | bytes 417792
  490.5 57.2 %collective-permute-start.6 = (bf16[1024,384]{1,0:T(8,128)(2,1)}, bf16[1024,384]{1,0:T(8,128)(2,1)S(1)}, u32[]{:S(2)}, u32[]{:S(2)}) collective-permute-start(bf16[1024,384]{1,0:T(8,128)(2,1)} %get-tuple-element.52), channel_id=1, source_target_pairs={{0,2},{2,0},{1,3},{3,1},{4,6},{6,4},{5,7},{7,5},{8,10},{10,8},{9,1... | collective-permute-start | bytes 2359304 | tf_op jit(solution)/shard_map/ppermute | solution.py:584
  493.6 54.1 %copy-start.21 = (f32[1280,384]{1,0:T(8,128)S(1)}, f32[1280,384]{1,0:T(8,128)}, u32[]{:S(2)}) copy-start(f32[1280,384]{1,0:T(8,128)} %get-tuple-element.51) | copy-start | bytes 5898244
  494.9 53.1 %copy-start.27 = (bf16[256,384]{1,0:T(8,128)(2,1)S(1)}, bf16[256,384]{1,0:T(8,128)(2,1)}, u32[]{:S(2)}) copy-start(bf16[256,384]{1,0:T(8,128)(2,1)} %slice.265) | copy-start | bytes 589828
  550.6 13.0 %collective-permute-start.7 = (bf16[1280,768]{1,0:T(8,128)(2,1)}, bf16[1280,768]{1,0:T(8,128)(2,1)}, u32[]{:S(2)}, u32[]{:S(2)}) collective-permute-start(bf16[1280,768]{1,0:T(8,128)(2,1)} %fusion.19), channel_id=1, source_target_pairs={{0,1},{1,0},{2,3},{3,2},{4,5},{5,4},{6,7},{7,6},{8,9},{9,8},{10,11... | collective-permute-start | bytes 5898248 | tf_op jit(solution)/shard_map/ppermute | solution.py:584
  580.7 22.2 %collective-permute-start.8 = (bf16[3,8,48,384]{3,2,1,0:T(8,128)(2,1)S(1)}, bf16[3,8,48,384]{3,2,1,0:T(8,128)(2,1)}, u32[]{:S(2)}, u32[]{:S(2)}) collective-permute-start(bf16[3,8,48,384]{3,2,1,0:T(8,128)(2,1)S(1)} %fusion.68), channel_id=1, source_target_pairs={{0,2},{2,0},{1,3},{3,1},{4,6},{6,4},{5,7},{7,5},{8,10},{10,8},{9,1... | collective-permute-start | bytes 2654216 | tf_op jit(solution)/shard_map/ppermute | solution.py:584
  604.9 7.1 copy-start.39
  604.9 7.1 copy-start.38
  604.9 7.1 copy-start.35
  605.9 115.6 %all-to-all-start.8 = ((bf16[8,3,48,384]{3,2,1,0:T(8,128)(2,1)}), bf16[8,3,48,384]{3,2,1,0:T(8,128)(2,1)S(1)}, u32[]{:S(2)}, u32[]{:S(2)}) async-start(bf16[8,3,48,384]{3,2,1,0:T(8,128)(2,1)} %copy.49), calls=%async_computation.8 | async-start | bytes 1769472 | tf_op jit(solution)/shard_map/all_to_all | solution.py:604
  (48 other events, 107.2 us)
Sparse Core Ops, SparseCore 0:
  10.2 48.6 all-gather.5
  60.4 91.9 all-gather.9
  153.9 63.7 all-gather.7
  592.5 126.8 reduce-scatter.3

commit v2 on v0

--- a/solution.py
+++ b/solution.py
@@ -3,6 +3,8 @@
 import jax
 import jax.numpy as jnp
 from jax import lax
+from jax.experimental import pallas as pl
+from jax.experimental.pallas import tpu as pltpu
 from jax.sharding import PartitionSpec as P
 
 HEAD_DIM = 64
@@ -106,7 +108,7 @@
     return (query_grad, keys_grad, values_grad)
 
 
-def shards(
+def shards_any(
     tokens,
     cotangent,
     routes,
@@ -329,7 +331,735 @@
     )
 
 
+F32 = jnp.float32
+BF = jnp.bfloat16
+NT = (((1,), (1,)), ((), ()))
+TN = (((0,), (0,)), ((), ()))
+TILE = 256
+PAIR = 2 * HEAD_DIM
+
+
+def nt(a, b):
+    return lax.dot_general(a, b, NT, preferred_element_type=F32)
+
+
+def tn(a, b):
+    return lax.dot_general(a, b, TN, preferred_element_type=F32)
+
+
+def mm(a, b):
+    return jnp.dot(a, b, preferred_element_type=F32)
+
+
+def head_masks(rows):
+    lane = lax.broadcasted_iota(jnp.int32, (rows, PAIR), 1)
+    return (lane < HEAD_DIM, lane >= HEAD_DIM)
+
+
+def self_forward(q_ref, k_ref, v_ref, o_ref, lse_ref):
+    rows = q_ref.shape[0]
+    lo, hi = head_masks(TILE)
+    tri = lax.broadcasted_iota(jnp.int32, (TILE, TILE), 1) <= lax.broadcasted_iota(
+        jnp.int32, (TILE, TILE), 0
+    )
+    for i in range(rows // TILE):
+        at = pl.ds(i * TILE, TILE)
+        q = q_ref[at, :] * jnp.asarray(HEAD_DIM**-0.5, BF)
+        outs, lses = [], []
+        for mask in (lo, hi):
+            qm = jnp.where(mask, q, jnp.zeros_like(q))
+            diag = jnp.where(tri, nt(qm, k_ref[at, :]), NEG)
+            top = jnp.max(diag, axis=1, keepdims=True)
+            if i:
+                off = nt(qm, k_ref[: i * TILE, :])
+                top = jnp.maximum(top, jnp.max(off, axis=1, keepdims=True))
+            near = jnp.exp(diag - top)
+            total = jnp.sum(near, axis=1, keepdims=True)
+            acc = mm(near.astype(BF), v_ref[at, :])
+            if i:
+                early = jnp.exp(off - top)
+                total = total + jnp.sum(early, axis=1, keepdims=True)
+                acc = acc + mm(early.astype(BF), v_ref[: i * TILE, :])
+            outs.append(acc / total)
+            lses.append(top + jnp.log(total))
+        o_ref[at, :] = jnp.where(lo, outs[0], outs[1])
+        lse_ref[at, :] = jnp.where(lo, lses[0], lses[1])
+
+
+def cross_forward(word_ref, q_ref, k_ref, v_ref, o_ref, lse_ref, *rest):
+    ctx_ref, log_ref = rest[-2:]
+    rows = q_ref.shape[0]
+    lo, hi = head_masks(TILE)
+
+    def put(i, o, lse):
+        at = pl.ds(i * TILE, TILE)
+        ctx_ref[at, :] = o.astype(BF)
+        flipped = lse.T
+        log_ref[0:1, at] = flipped[0:1, :]
+        log_ref[1:2, at] = flipped[HEAD_DIM : HEAD_DIM + 1, :]
+
+    def tile(i):
+        at = pl.ds(i * TILE, TILE)
+        q = q_ref[at, :] * jnp.asarray(HEAD_DIM**-0.5, BF)
+        outs, lses = [], []
+        for mask in (lo, hi):
+            s = nt(jnp.where(mask, q, jnp.zeros_like(q)), k_ref[...])
+            top = jnp.max(s, axis=1, keepdims=True)
+            p = jnp.exp(s - top)
+            total = jnp.sum(p, axis=1, keepdims=True)
+            outs.append(mm(p.astype(BF), v_ref[...]) / total)
+            lses.append(top + jnp.log(total))
+        o_far = jnp.where(lo, outs[0], outs[1])
+        l_far = jnp.where(lo, lses[0], lses[1])
+        l_near = lse_ref[at, :]
+        top = jnp.maximum(l_near, l_far)
+        near, far = jnp.exp(l_near - top), jnp.exp(l_far - top)
+        both = near + far
+        put(i, (o_ref[at, :] * near + o_far * far) / both, top + jnp.log(both))
+
+    def keep(i):
+        at = pl.ds(i * TILE, TILE)
+        put(i, o_ref[at, :], lse_ref[at, :])
+
+    later = word_ref[0] == 1
+    for i in range(rows // TILE):
+        if i >= k_ref.shape[0] // TILE:
+            tile(i)
+        else:
+            pl.when(later)(partial(tile, i))
+            pl.when(jnp.logical_not(later))(partial(keep, i))
+
+
+def row_dots(g, o):
+    prod = (g.astype(F32) * o.astype(F32)).T
+    return (
+        jnp.sum(prod[:HEAD_DIM], axis=0, keepdims=True),
+        jnp.sum(prod[HEAD_DIM:], axis=0, keepdims=True),
+    )
+
+
+def pair_back(q, g, k, v, kt, lse, dots, masks, visible):
+    ps, ds, qs, gs, dq = [], [], [], [], []
+    for h in range(2):
+        qm = jnp.where(masks[h], q, jnp.zeros_like(q))
+        gm = jnp.where(masks[h], g, jnp.zeros_like(g))
+        p = jnp.exp(nt(k, qm) - lse[h])
+        if visible is not None:
+            p = jnp.where(visible, p, 0.0)
+        d = (p * (nt(v, gm) - dots[h])).astype(BF)
+        ps.append(p.astype(BF))
+        ds.append(d)
+        qs.append(qm)
+        gs.append(gm)
+        dq.append(mm(kt[h * HEAD_DIM : (h + 1) * HEAD_DIM, :], d))
+    dv = mm(jnp.concatenate(ps, axis=1), jnp.concatenate(gs, axis=0))
+    dk = mm(jnp.concatenate(ds, axis=1), jnp.concatenate(qs, axis=0))
+    return jnp.concatenate(dq, axis=0), dk, dv
+
+
+def cross_backward(word_ref, q_ref, k_ref, v_ref, g_ref, c_ref, log_ref, dq_ref, dkv_ref, dk_acc, dv_acc):
+    rows, keys = q_ref.shape[0], k_ref.shape[0]
+    masks = head_masks(TILE)
+    dk_acc[...] = jnp.zeros_like(dk_acc)
+    dv_acc[...] = jnp.zeros_like(dv_acc)
+    kt = k_ref[...].T
+
+    def tile(i):
+        at = pl.ds(i * TILE, TILE)
+        q = q_ref[at, :] * jnp.asarray(HEAD_DIM**-0.5, BF)
+        g = g_ref[at, :]
+        dots = row_dots(g, c_ref[at, :])
+        lse = (log_ref[0:1, at], log_ref[1:2, at])
+        dq, dk, dv = pair_back(q, g, k_ref[...], v_ref[...], kt, lse, dots, masks, None)
+        dq_ref[:, at] = dq
+        dk_acc[...] += dk
+        dv_acc[...] += dv
+
+    def skip(i):
+        dq_ref[:, pl.ds(i * TILE, TILE)] = jnp.zeros((PAIR, TILE), F32)
+
+    later = word_ref[0] == 1
+    for i in range(rows // TILE):
+        if i >= keys // TILE:
+            tile(i)
+        else:
+            pl.when(later)(partial(tile, i))
+            pl.when(jnp.logical_not(later))(partial(skip, i))
+    dkv_ref[:, :PAIR] = dk_acc[...].astype(BF)
+    dkv_ref[:, PAIR:] = dv_acc[...].astype(BF)
+
+
+def self_backward(q_ref, k_ref, v_ref, g_ref, c_ref, log_ref, dqx_ref, far_ref, *rest):
+    out_ref, dk_acc, dv_acc = rest[-3:]
+    rows, keys = q_ref.shape[0], far_ref.shape[0]
+    masks = head_masks(TILE)
+    dk_acc[:keys, :] = far_ref[:, :PAIR].astype(F32)
+    dv_acc[:keys, :] = far_ref[:, PAIR:].astype(F32)
+    dk_acc[keys:, :] = jnp.zeros((rows - keys, PAIR), F32)
+    dv_acc[keys:, :] = jnp.zeros((rows - keys, PAIR), F32)
+    kt = k_ref[...].T
+    seen = lax.broadcasted_iota(jnp.int32, (TILE, TILE), 0) <= lax.broadcasted_iota(
+        jnp.int32, (TILE, TILE), 1
+    )
+    for i in range(rows // TILE):
+        at = pl.ds(i * TILE, TILE)
+        q = q_ref[at, :] * jnp.asarray(HEAD_DIM**-0.5, BF)
+        g = g_ref[at, :]
+        dots = row_dots(g, c_ref[at, :])
+        lse = (log_ref[0:1, at], log_ref[1:2, at])
+        dq, dk, dv = pair_back(
+            q, g, k_ref[at, :], v_ref[at, :], kt[:, i * TILE : (i + 1) * TILE], lse, dots, masks, seen
+        )
+        dk_acc[at, :] += dk
+        dv_acc[at, :] += dv
+        if i:
+            n = i * TILE
+            dq_early, dk, dv = pair_back(
+                q, g, k_ref[:n, :], v_ref[:n, :], kt[:, :n], lse, dots, masks, None
+            )
+            dq = dq + dq_early
+            dk_acc[:n, :] += dk
+            dv_acc[:n, :] += dv
+        out_ref[at, :PAIR] = ((dq + dqx_ref[:, at]) * (HEAD_DIM**-0.5)).T.astype(BF)
+    out_ref[:, PAIR : 2 * PAIR] = dk_acc[...].astype(BF)
+    out_ref[:, 2 * PAIR :] = dv_acc[...].astype(BF)
+
+
+def column(rows, width, at):
+    return pl.BlockSpec((rows, width), lambda *_: (0, at))
+
+
+ANY = pl.BlockSpec(memory_space=pl.ANY)
+
+
+def shape(dims, dtype):
+    return jax.ShapeDtypeStruct(dims, dtype)
+
+
+def cost(elements, matmuls):
+    return pl.CostEstimate(
+        flops=2 * elements * PAIR * matmuls, transcendentals=elements, bytes_accessed=4 * 1280 * 1024
+    )
+
+
+def run_self_forward(qkv, width):
+    rows = qkv.shape[0]
+    spec = lambda j: pl.BlockSpec((rows, PAIR), lambda p: (0, 3 * p + j))
+    out = pl.BlockSpec((rows, PAIR), lambda p: (0, p))
+    return pl.pallas_call(
+        self_forward,
+        grid=(width // PAIR,),
+        in_specs=[spec(0), spec(1), spec(2)],
+        out_specs=[out, out],
+        out_shape=[shape((rows, width), F32)] * 2,
+        cost_estimate=cost(6 * rows * rows, 4),
+        name="self_forward",
+    )(qkv, qkv, qkv)
+
+
+def run_cross_forward(p, word, qkv, far, out, lse, carried):
+    rows, width = out.shape
+    keys = far.shape[0]
+    return pl.pallas_call(
+        cross_forward,
+        grid_spec=pltpu.PrefetchScalarGridSpec(
+            num_scalar_prefetch=1,
+            grid=(1,),
+            in_specs=[
+                column(rows, PAIR, 3 * p),
+                column(keys, PAIR, 0),
+                column(keys, PAIR, 1),
+                column(rows, PAIR, p),
+                column(rows, PAIR, p),
+            ]
+            + [ANY] * len(carried),
+            out_specs=[
+                column(rows, PAIR, p),
+                pl.BlockSpec((None, 2, rows), lambda *_: (p, 0, 0)),
+            ],
+        ),
+        out_shape=[shape((rows, width), BF), shape((width // PAIR, 2, rows), F32)],
+        input_output_aliases={6 + i: i for i in range(len(carried))},
+        cost_estimate=cost(2 * rows * keys, 4),
+        name=f"cross_forward_{p}",
+    )(word, qkv, far, far, out, lse, *carried)
+
+
+def run_cross_backward(p, word, qkv, far, g, context, log_rows):
+    rows = g.shape[0]
+    keys = far.shape[0]
+    return pl.pallas_call(
+        cross_backward,
+        grid_spec=pltpu.PrefetchScalarGridSpec(
+            num_scalar_prefetch=1,
+            grid=(1,),
+            in_specs=[
+                column(rows, PAIR, 3 * p),
+                column(keys, PAIR, 0),
+                column(keys, PAIR, 1),
+                column(rows, PAIR, p),
+                column(rows, PAIR, p),
+                pl.BlockSpec((None, 2, rows), lambda *_: (p, 0, 0)),
+            ],
+            out_specs=[column(PAIR, rows, 0), column(keys, 2 * PAIR, 0)],
+            scratch_shapes=[pltpu.VMEM((keys, PAIR), F32)] * 2,
+        ),
+        out_shape=[shape((PAIR, rows), F32), shape((keys, 2 * PAIR), BF)],
+        cost_estimate=cost(2 * rows * keys, 8),
+        name=f"cross_backward_{p}",
+    )(word, qkv, far, far, g, context, log_rows)
+
+
+def run_self_backward(p, qkv, g, context, log_rows, far_query, far, carried):
+    rows, width = g.shape
+    keys = far.shape[0]
+    return pl.pallas_call(
+        self_backward,
+        grid=(1,),
+        in_specs=[
+            column(rows, PAIR, 3 * p),
+            column(rows, PAIR, 3 * p + 1),
+            column(rows, PAIR, 3 * p + 2),
+            column(rows, PAIR, p),
+            column(rows, PAIR, p),
+            pl.BlockSpec((None, 2, rows), lambda *_: (p, 0, 0)),
+            column(PAIR, rows, 0),
+            column(keys, 2 * PAIR, 0),
+        ]
+        + [ANY] * len(carried),
+        out_specs=column(rows, 3 * PAIR, p),
+        out_shape=shape((rows, 3 * width), BF),
+        scratch_shapes=[pltpu.VMEM((rows, PAIR), F32)] * 2,
+        input_output_aliases={8: 0} if carried else {},
+        cost_estimate=cost(rows * rows, 8),
+        name=f"self_backward_{p}",
+    )(qkv, qkv, qkv, g, context, log_rows, far_query, far, *carried)
+
+
+ROOT_HALF = 0.7071067811865476
+DENSITY = 0.3989422804014327
+
+
+def quarter_of(j, word):
+    return 2 * (word[0] ^ 1 ^ (j & 1)) + (word[1] ^ 1 ^ (j >> 1))
+
+
+def expert_step(index, word_ref, x_ref, cot_ref, *refs):
+    ups, downs, vec_ref = refs[:4], refs[4:8], refs[8]
+    carried = 2 * index
+    sent_ref, small_ref, dx_ref, gu_ref, ku_ref, gd_ref, kd_ref = refs[9 + carried : 16 + carried]
+    rg, xt, gate, res, dx, up, down = refs[16 + carried :]
+    small_in = refs[10] if index else None
+    j = pl.program_id(0)
+    rows, width = x_ref.shape
+    thin = width // 4
+    cut = down.shape[0]
+    ff = 4 * cut
+    bias_at = pl.ds(pl.multiple_of(quarter_of(j, word_ref) * cut, cut), cut)
+    down_bias = vec_ref[0:1, ff : ff + width].astype(F32)
+    centre = vec_ref[0:1, ff + width :].astype(F32)
+
+    @pl.when(j == 0)
+    def _():
+        x = x_ref[...]
+        score = jnp.sum(x.astype(F32) * centre, axis=1, keepdims=True)
+        g = jax.nn.sigmoid(score)
+        gate[...] = jnp.broadcast_to(g, gate.shape)
+        r = (g * cot_ref[...].reshape(rows, width).astype(F32)).astype(BF)
+        rg[...] = r
+        small_ref[...] = small_in[...] if index else jnp.zeros_like(small_ref)
+        small_ref[2:3, index * width : (index + 1) * width] = jnp.sum(
+            r.astype(F32), axis=0, keepdims=True
+        )
+        t = x.T
+        for s in range(4):
+            at = 2 * (1 ^ word_ref[1] ^ (s & 1)) + (1 ^ word_ref[0] ^ (s >> 1))
+            xt[pl.ds(pl.multiple_of(at * thin, thin), thin), :] = t[s * thin : (s + 1) * thin, :]
+        res[...] = jnp.zeros_like(res)
+        dx[...] = jnp.zeros_like(dx)
+
+    for k in range(4):
+        at = quarter_of(k, word_ref)
+        up[pl.ds(pl.multiple_of(at * thin, thin), thin), :] = ups[k][...]
+
+        @pl.when(j == k)
+        def _():
+            down[...] = downs[k][...]
+
+    r = rg[...]
+    inner = mm(x_ref[...], up[...]) + vec_ref[0:1, bias_at].astype(F32)
+    cdf = 0.5 * (1.0 + lax.erf(inner * ROOT_HALF))
+    hidden = (inner * cdf).astype(BF)
+    slope = cdf + inner * (jnp.exp(-0.5 * inner * inner) * DENSITY)
+    res[...] += mm(hidden, down[...])
+    back = (nt(r, down[...]) * slope).astype(BF)
+    small_ref[index : index + 1, bias_at] = jnp.sum(back.astype(F32), axis=0, keepdims=True)
+    dx[...] += nt(back, up[...])
+    grad = mm(xt[...], back)
+    gu_ref[...] = grad[: 2 * thin].astype(BF)
+    ku_ref[...] = grad[2 * thin :].astype(BF)
+    grad = tn(hidden, r).astype(BF)
+
+    @pl.when(j < 2)
+    def _():
+        gd_ref[...] = grad
+
+    @pl.when(j >= 2)
+    def _():
+        kd_ref[...] = grad
+
+    @pl.when(j == 3)
+    def _():
+        g = gate[:, :1]
+        out = res[...] + down_bias
+        sent_ref[...] = (g * out).astype(BF).reshape(sent_ref.shape)
+        cot = cot_ref[...].reshape(rows, width).astype(F32)
+        sg = jnp.sum(cot * out, axis=1, keepdims=True) * g * (1.0 - g)
+        sg = sg.astype(BF).astype(F32)
+        dx_ref[...] = (dx[...] + sg * centre).astype(BF)
+        small_ref[2:3, (2 + index) * width : (3 + index) * width] = jnp.sum(
+            sg * x_ref[...].astype(F32), axis=0, keepdims=True
+        )
+
+
+def run_expert(index, word, x, cot, ups, downs, vectors, carried):
+    rows, width = x.shape
+    owners, experts, capacity, _ = cot.shape
+    ff = ups[0].shape[2]
+    cut, thin = ff // 4, width // 4
+    whole = lambda *dims: pl.BlockSpec(dims, lambda j, w: (0,) * len(dims))
+    slot = pl.BlockSpec((owners, None, capacity, width), lambda j, w: (0, index, 0, 0))
+    upper = pl.BlockSpec((2, thin, cut), lambda j, w: (0, 0, quarter_of(j, w)))
+    half_up = pl.BlockSpec((2 * thin, cut), lambda j, w: (0, quarter_of(j, w)))
+    assert experts == 2
+    return pl.pallas_call(
+        partial(expert_step, index),
+        grid_spec=pltpu.PrefetchScalarGridSpec(
+            num_scalar_prefetch=1,
+            grid=(4,),
+            in_specs=[whole(rows, width), slot]
+            + [pl.BlockSpec((None, thin, cut), lambda j, w: (index, 0, quarter_of(j, w)))] * 4
+            + [pl.BlockSpec((None, cut, width), lambda j, w: (index, 0, 0))] * 4
+            + [pl.BlockSpec((None, 1, ff + 2 * width), lambda j, w: (index, 0, 0))]
+            + ([ANY, whole(8, ff)] if carried else []),
+            out_specs=[
+                slot,
+                whole(8, ff),
+                whole(rows, width),
+                half_up,
+                half_up,
+                pl.BlockSpec((None, cut, width), lambda j, w: (jnp.minimum(j, 1), 0, 0)),
+                pl.BlockSpec((None, cut, width), lambda j, w: (jnp.maximum(j, 2) - 2, 0, 0)),
+            ],
+            scratch_shapes=[
+                pltpu.VMEM((rows, width), BF),
+                pltpu.VMEM((width, rows), BF),
+                pltpu.VMEM((rows, 128), F32),
+                pltpu.VMEM((rows, width), F32),
+                pltpu.VMEM((rows, width), F32),
+                pltpu.VMEM((width, cut), BF),
+                pltpu.VMEM((cut, width), BF),
+            ],
+        ),
+        out_shape=[
+            shape(cot.shape, BF),
+            shape((8, ff), F32),
+            shape((rows, width), BF),
+            shape((2 * thin, ff), BF),
+            shape((2 * thin, ff), BF),
+            shape((2, cut, width), BF),
+            shape((2, cut, width), BF),
+        ],
+        input_output_aliases={12: 0} if carried else {},
+        cost_estimate=pl.CostEstimate(
+            flops=12 * rows * width * ff, transcendentals=2 * rows * ff, bytes_accessed=24 << 20
+        ),
+        name=f"expert_{index}",
+    )(word, x, cot, *ups, *downs, vectors, *carried)
+
+
+SWAP = ((0, 1), (1, 0))
+
+
+def swap(value, axis):
+    return lax.ppermute(value, axis, SWAP)
+
+
+def after(value, *others):
+    return lax.optimization_barrier((value,) + others)[0]
+
+
+def spread_rows(value, axis=0):
+    return lax.all_to_all(value, "fsdp", split_axis=axis, concat_axis=axis, tiled=True)
+
+
+def scope(name):
+    return jax.named_scope(name)
+
+
+def shards_pair(
+    tokens,
+    cotangent,
+    routes,
+    qkv_weight,
+    out_weight,
+    layer_norm_gains,
+    layer_norm_biases,
+    up_weight,
+    up_shift,
+    down_weight,
+    down_shift,
+    centroids,
+):
+    block, width = tokens.shape[2:]
+    pslice = block - LEN
+    half = routes.shape[2]
+    experts, thin, ff = up_weight.shape
+    cut = down_weight.shape[1]
+    owners = lax.axis_size("fsdp")
+    place = lax.axis_index("ctx")
+    side = lax.axis_index("tp")
+    half_start = side * half
+    word = jnp.stack([place, side]).astype(jnp.int32)
+    local = qkv_weight.shape[2]
+    pairs = local // PAIR
+
+    def own_half(value):
+        return lax.dynamic_slice_in_dim(value, half_start, half, 0)
+
+    def other_half(value):
+        return lax.dynamic_slice_in_dim(value, half - half_start, half, 0)
+
+    def join_halves(own):
+        other = swap(own, "tp")
+        buffer = jnp.zeros((block, width), own.dtype)
+        buffer = lax.dynamic_update_slice_in_dim(buffer, own, half_start, 0)
+        return lax.dynamic_update_slice_in_dim(buffer, other, half - half_start, 0)
+
+    packed = qkv_weight.reshape(3, -1, pairs, PAIR).transpose(1, 2, 0, 3).reshape(-1, 3 * local)
+    with scope("gather_qkv"):
+        project = lax.all_gather(packed, "fsdp", axis=0, tiled=True)
+    with scope("gather_out"):
+        output = lax.all_gather(out_weight.T, "fsdp", axis=0, tiled=True)
+    with scope("up_ctx"):
+        up_far = swap(up_weight, "ctx")
+
+    rows_in = tokens.reshape(block, width)
+    first_rows, first_standard, first_spread = norm_input_rows(
+        rows_in.astype(F32), layer_norm_gains[0], layer_norm_biases[0]
+    )
+    first = first_rows.astype(BF)
+    projected = jnp.dot(first, project, preferred_element_type=F32).astype(BF)
+    far = []
+    for p in range(pairs):
+        start = (3 * p + 1) * PAIR
+        with scope(f"far_{p}"):
+            far.append(swap(projected[:pslice, start : start + 2 * PAIR], "ctx"))
+
+    with scope("down_ctx"):
+        down_far = swap(after(down_weight, far[0]), "ctx")
+    vector = jnp.concatenate([up_shift, down_shift, centroids], axis=1)
+    vector_far = swap(vector, "ctx")
+    with scope("up_tp"):
+        up_side, up_both = swap(up_weight, "tp"), swap(up_far, "tp")
+    with scope("down_tp"):
+        down_side, down_both = swap(down_weight, "tp"), swap(down_far, "tp")
+    vector_side, vector_both = swap(vector, "tp"), swap(vector_far, "tp")
+    ups = (up_both, up_side, up_far, up_weight)
+    downs = (down_both, down_side, down_far, down_weight)
+    by_quarter = [
+        jnp.where(
+            side == s % 2,
+            jnp.where(place == s // 2, vector, vector_far),
+            jnp.where(place == s // 2, vector_side, vector_both),
+        )
+        for s in range(4)
+    ]
+    vectors = jnp.concatenate(
+        [v[:, :cut] for v in by_quarter]
+        + [v[:, cut : cut + thin] for v in by_quarter]
+        + [v[:, cut + thin :] for v in by_quarter],
+        axis=1,
+    )[:, None]
+
+    route = routes.reshape(half)
+    total_experts = experts * owners
+    capacity = 2 * half // total_experts
+    member = (route[:, None] == lax.broadcasted_iota(jnp.int32, (half, total_experts), 1)).astype(
+        jnp.int32
+    )
+    rank = jnp.sum((jnp.cumsum(member, axis=0) - 1) * member, axis=1)
+    slot_of = (route // experts) * capacity + rank
+    slots = lax.broadcasted_iota(jnp.int32, (owners * capacity, half), 0)
+    placing = [
+        ((slots == slot_of[None, :]) & (route % experts == e)[None, :]).astype(BF)
+        for e in range(experts)
+    ]
+
+    def to_slots(e, rows):
+        spread = jnp.dot(placing[e], rows, preferred_element_type=F32).astype(BF)
+        return spread.reshape(owners, capacity, width)
+
+    def from_slots(parts):
+        return sum(
+            lax.dot_general(m, part, TN, preferred_element_type=F32)
+            for m, part in zip(placing, parts)
+        )
+
+    upstream_half = own_half(cotangent.reshape(block, width))
+    with scope("cot_out"):
+        arrived_grad = spread_rows(
+            jnp.stack([to_slots(e, upstream_half) for e in range(experts)], axis=1)
+        )
+
+    near_out, near_log = run_self_forward(projected, local)
+    carried = ()
+    for p in range(pairs):
+        carried = run_cross_forward(p, word, projected, far[p], near_out, near_log, carried)
+    context, log_rows = carried
+
+    sent_half = lax.dot_general(other_half(context), output, NT, preferred_element_type=F32)
+    kept_half = lax.dot_general(own_half(context), output, NT, preferred_element_type=F32)
+    with scope("attended_tp"):
+        received = swap(sent_half.astype(BF), "tp")
+    resid = own_half(rows_in).astype(F32) + kept_half + received.astype(F32)
+    second_rows, second_standard, second_spread = norm_input_rows(
+        resid, layer_norm_gains[1], layer_norm_biases[1]
+    )
+    second = second_rows.astype(BF)
+    arrived = []
+    for e in range(experts):
+        with scope(f"rows_out_{e}"):
+            arrived.append(spread_rows(to_slots(e, second)).reshape(owners * capacity, width))
+
+    returned, crossing = [], []
+    carried = ()
+    for e in range(experts):
+        with scope(f"expert_{e}"):
+            sent, small, rows_grad, gu, ku, gd, kd = run_expert(
+                e, word, arrived[e], arrived_grad, ups, downs, vectors, carried
+            )
+        carried = (sent, small)
+        with scope(f"rows_back_{e}"):
+            returned.append(
+                spread_rows(rows_grad.reshape(owners, capacity, width)).reshape(-1, width)
+            )
+        sums = []
+        for name, give, keep in (("up", gu, ku), ("down", gd, kd)):
+            dims = (2, thin, ff) if name == "up" else (2, cut, width)
+            give, keep = give.reshape(dims), keep.reshape(dims)
+            with scope(f"{name}_grad_tp_{e}"):
+                sums.append((keep, swap(give, "tp")))
+        crossing.append(sums)
+
+    half_grad = from_slots(returned).astype(BF).astype(F32)
+    norm_grad, gain_two, shift_two = norm_back(
+        half_grad, second_standard, second_spread, layer_norm_gains[1]
+    )
+    attended_half = (upstream_half.astype(F32) + norm_grad).astype(BF)
+    with scope("attended_grad_tp"):
+        attended_grad = join_halves(attended_half)
+
+    with scope("output_back"):
+        sent = spread_rows(sent).transpose(1, 0, 2, 3).reshape(experts, owners * capacity, width)
+    expert_half = from_slots([sent[e] for e in range(experts)])
+    with scope("mixed_tp"):
+        mixed = join_halves((resid + expert_half).astype(BF))
+
+    def sum_owners(value):
+        value = spread_rows(value.astype(BF).reshape(owners, -1, local))
+        return jnp.sum(value.astype(F32), axis=0)
+
+    context_grad = jnp.dot(attended_grad, output, preferred_element_type=F32).astype(BF)
+    far_query, far_back = [], []
+    for p in range(pairs):
+        query, pair_grad = run_cross_backward(
+            p, word, projected, far[p], context_grad, context, log_rows
+        )
+        far_query.append(query)
+        with scope(f"far_back_{p}"):
+            far_back.append(swap(pair_grad, "ctx"))
+    projection_sums = []
+    with scope("out_sum"):
+        projection_sums.append(
+            sum_owners(
+                lax.dot_general(attended_grad, context, TN, preferred_element_type=F32)
+            )
+        )
+
+    def cross_sum(e, at):
+        keep, got = crossing[e][at]
+        first_sum = (keep[0].astype(F32) + got[0].astype(F32)).astype(BF)
+        if e:
+            first_sum = after(first_sum, far_back[-2])
+        with scope(f"grad_ctx_{e}_{at}"):
+            crossed = swap(first_sum, "ctx")
+        return keep[1].astype(F32) + got[1].astype(F32) + crossed.astype(F32)
+
+    up_grad, down_grad = (
+        jnp.stack([cross_sum(e, at) for e in range(experts)]) for at in range(2)
+    )
+    small = small + swap(small, "tp")
+    small = small + swap(small, "ctx")
+    quarter = place * 2 + side
+    up_shift_grad = lax.dynamic_slice(small, (0, quarter * cut), (experts, cut))
+    vectors_grad = lax.dynamic_slice(
+        small[2].reshape(2 * experts, width), (0, quarter * thin), (2 * experts, thin)
+    )
+
+    grads = ()
+    for p in range(pairs):
+        grads = run_self_backward(
+            p, projected, context_grad, context, log_rows, far_query[p], far_back[p], grads
+        )
+        pair = grads[:, 3 * PAIR * p : 3 * PAIR * (p + 1)]
+        with scope(f"qkv_sum_{p}"):
+            projection_sums.append(
+                sum_owners(lax.dot_general(first, pair, TN, preferred_element_type=F32))
+            )
+        grads = (grads,)
+    grads = grads[0]
+
+    first_part = lax.dot_general(grads, project, NT, preferred_element_type=F32).astype(BF)
+    with scope("first_tp"):
+        first_grad = first_part.astype(F32) + swap(first_part, "tp").astype(F32)
+    stream_grad, gain_one, shift_one = norm_back(
+        first_grad, first_standard, first_spread, layer_norm_gains[0]
+    )
+    tokens_grad = attended_grad.astype(F32) + stream_grad
+
+    sums = jnp.stack(projection_sums).reshape(1 + pairs, 2, -1, local)
+    give = lax.dynamic_index_in_dim(sums, 1 - place, 1, keepdims=False).astype(BF)
+    keep = lax.dynamic_index_in_dim(sums, place, 1, keepdims=False)
+    with scope("sums_ctx"):
+        total = keep + swap(give, "ctx").astype(F32)
+    out_grad = total[0].T
+    qkv_grad = total[1:].reshape(pairs, -1, 3, PAIR).transpose(2, 1, 0, 3).reshape(3, -1, local)
+
+    two = jnp.stack([gain_two, shift_two])
+    two = two + swap(two, "tp")
+    norms = jnp.stack([gain_one, two[0], shift_one, two[1]]).reshape(4, owners, -1)
+    norms = jnp.sum(spread_rows(norms.transpose(1, 0, 2)), axis=0)
+    norms = norms + swap(norms, "ctx")
+    piece = width // (2 * owners)
+    norms = lax.dynamic_slice(norms, (0, place * piece), (4, piece))
+    return (
+        mixed.reshape(1, 1, block, width),
+        tokens_grad.reshape(1, 1, block, width),
+        qkv_grad,
+        out_grad,
+        norms[:2],
+        norms[2:],
+        up_grad,
+        up_shift_grad,
+        down_grad,
+        vectors_grad[:experts],
+        vectors_grad[experts:],
+    )
+
+
 def solution(mesh):
+    paired = mesh.shape["ctx"] == 2 and mesh.shape["tp"] == 2
     in_specs = (
         P("fsdp", "ctx", None, None),
         P("fsdp", "ctx", None, None),
@@ -357,4 +1087,5 @@
         P("fsdp", ("ctx", "tp")),
         P("fsdp", ("ctx", "tp")),
     )
-    return jax.shard_map(shards, mesh=mesh, in_specs=in_specs, out_specs=out_specs, check_vma=False)
+    return jax.shard_map(
+        shards_pair if paired else shards_any, mesh=mesh, in_specs=in_specs, out_specs=out_specs, check_vma=False)

time: 1500 us -> 596 us (0.40)
  waiting for transfers between devices: 872 us -> 125 us
  matrix products: 344 us -> 50 us
  Pallas kernels: 0 us -> 136 us
  starting transfers between devices: 15.9 us -> 86.3 us
  local copies, waits for them, and re-layouts: 73.5 us -> 39.7 us
  blocking collectives: 101 us -> 82.6 us
    unnamed x26 -> x1, waiting for transfers between devices: 427 us -> 0.02 us
    reduce_scatter x5 -> x0, waiting for transfers between devices: 323 us -> none  [the longest x1 126 us: shards(): lax.psum_scatter(output_grad, ('fsdp', 'ctx'), scatter_dimension=1, tiled...]
    dot_general x60 -> x17, matrix products: 344 us -> 50 us  [the longest x3 11.5 us: shards_pair(): lax.dot_general(first, pair, TN, preferred_element_type=F32)]
    pallas_call x0 -> x12, Pallas kernels: none -> 136 us  [the longest x2 62.1 us: run_expert(): pl.pallas_call(partial(expert_step, index), grid_spec=pltpu.PrefetchScala...]
    ppermute x0 -> x32, waiting for transfers between devices: none -> 82 us  [swap(): return lax.ppermute(value, axis, SWAP)]
    all_gather x7 -> x1, waiting for transfers between devices: 65.8 us -> 0.01 us  [shards_pair(): project = lax.all_gather(packed, 'fsdp', axis=0, tiled=True)]
    all_to_all x1 -> x0, blocking collectives: 51.3 us -> none  [shards(): lax.all_to_all(rows_grad.astype(jnp.bfloat16), 'fsdp', split_axis=0, conc...]
    all_to_all x3 -> x11, starting transfers between devices: 15.1 us -> 58.7 us  [spread_rows(): lax.all_to_all(value, 'fsdp', split_axis=axis, concat_axis=axis, tiled=True)]
  transfers between devices with their start and end apart: 23 -> 44, of which waited for: 14 -> 17; matrix products, arithmetic and copies ran while one was open for 11% -> 22% of each run, Pallas kernels for 0% -> 23%
where the time goes in v2:
time: 596 us; the launch traced here: 590 us
  Pallas kernels  136 us (23%)
  waiting for transfers between devices  125 us (21%)
  starting transfers between devices  86.3 us (14%)
  blocking collectives  82.6 us (14%)
  other arithmetic  54.3 us (9%)
  matrix products  50 us (8%)
  local copies, waits for them, and re-layouts  39.7 us (7%)
  between operations  15.2 us (3%)
    all_gather x1, blocking collectives, shards_pair(): output = lax.all_gather(out_weight.T, 'fsdp', axis=0, tiled=True)  82.6 us
    ppermute x32, waiting for transfers between devices, swap(): return lax.ppermute(value, axis, SWAP)  82 us
    pallas_call x2, Pallas kernels, run_expert(): pl.pallas_call(partial(expert_step, index), grid_spec=pltpu.PrefetchScala...  62.1 us
    all_to_all x11, starting transfers between devices, spread_rows(): lax.all_to_all(value, 'fsdp', split_axis=axis, concat_axis=axis, tiled=True)  58.7 us
    all_to_all x11, waiting for transfers between devices, spread_rows(): lax.all_to_all(value, 'fsdp', split_axis=axis, concat_axis=axis, tiled=True)  43.3 us
    pallas_call x3, Pallas kernels, run_self_backward(): pl.pallas_call(self_backward, grid=(1,), in_specs=[column(rows, PAIR, 3 *...  29.7 us
    ppermute x32, starting transfers between devices, swap(): return lax.ppermute(value, axis, SWAP)  27.6 us
    another operation x6, other arithmetic, shards_pair(): jnp.stack([cross_sum(e, at) for e in range(experts)])  17.7 us
  transfers between devices with their start and end apart: 44, of which 17 were waited for; matrix products, arithmetic and copies ran while one was open for 22% of the time, Pallas kernels for 23%

profile of v2, /device:TPU:0, one launch (start us, length us, event | category | flops | bytes accessed | tf_op | source)
XLA Modules:
  0.0 589.6 jit_solution(8787651929852871286)
XLA Ops:
  15.8 7.4 %all-to-all-start.1 = ((bf16[8,2,80,768]{3,2,1,0:T(8,128)(2,1)}), bf16[8,2,80,768]{3,2,1,0:T(8,128)(2,1)}, u32[]{:S(2)}, u32[]{:S(2)}) async-start(bf16[8,2,80,768]{3,2,1,0:T(8,128)(2,1)} %pad_maximum_fusion.2), calls=%async_computation.1 | async-start | bytes 3932160 | tf_op jit(solution)/shard_map/cot_out/all_to_all | solution.py:793
  27.6 82.6 %all_gather.7 = bf16[768,384]{1,0:T(8,128)(2,1)S(1)} all-gather(bf16[96,384]{1,0:T(8,128)(2,1)S(1)} %bitcast.186), channel_id=1, replica_groups=mesh['fsdp'=8,'ctx'=2,'tp'=2] {'fsdp'}, dimensions={0}, use_global_device_ids=true | all-gather | bytes 663552 | tf_op jit(solution)/shard_map/gather_out/all_gather | solution.py:843
  112.2 4.8 convolution_convert_fusion.q_ref.k_ref.v_ref
  121.8 15.7 %self_forward.1 = (f32[1280,384]{1,0:T(8,128)}, f32[1280,384]{1,0:T(8,128)}) custom-call(bf16[1280,1152]{1,0:T(8,128)(2,1)} %copy-done, bf16[1280,1152]{1,0:T(8,128)(2,1)} %copy-done, bf16[1280,1152]{1,0:T(8,128)(2,1)} %copy-done), custom_call_target="tpu_custom_call" | custom-call | flops 10066329600 | bytes 5242880 | tf_op jit(solution)/shard_map/self_forward/pallas_call | solution.py:549
  138.0 5.0 cross_forward_0.1
  144.6 4.5 cross_forward_1.1
  149.1 6.8 %collective-permute-done.k_ref.v_ref = bf16[1024,256]{1,0:T(8,128)(2,1)} collective-permute-done((bf16[1024,256]{1,0:T(8,128)(2,1)}, bf16[1024,256]{1,0:T(8,128)(2,1)}, u32[]{:S(2)}, u32[]{:S(2)}) %collective-permute-start) | collective-permute-done | bytes 524320 | tf_op jit(solution)/shard_map/far_2/ppermute | solution.py:785
  155.9 4.6 cross_forward_2.1
  167.3 32.5 %collective-permute-done.7.refs_6_ = bf16[2,768,768]{2,1,0:T(8,128)(2,1)} collective-permute-done((bf16[2,768,768]{2,1,0:T(8,128)(2,1)}, bf16[2,768,768]{2,1,0:T(8,128)(2,1)}, u32[]{:S(2)}, u32[]{:S(2)}) %collective-permute-start.7) | collective-permute-done | bytes 2359328 | tf_op jit(solution)/shard_map/down_ctx/ppermute | solution.py:785
  202.2 3.6 all-to-all-start.2
  216.7 3.2 fusion.55
  219.9 11.1 %all-to-all-done.2 = bf16[8,80,768]{2,1,0:T(8,128)(2,1)S(1)} async-done(((bf16[8,80,768]{2,1,0:T(8,128)(2,1)}), bf16[8,80,768]{2,1,0:T(8,128)(2,1)S(1)}, u32[]{:S(2)}, u32[]{:S(2)}) %all-to-all-start.2) | async-done | bytes 983072 | tf_op jit(solution)/shard_map/rows_out_0/all_to_all | solution.py:793
  231.0 4.4 all-to-all-start
  244.8 31.1 %expert_0.1 = (bf16[8,2,80,768]{3,2,1,0:T(8,128)(2,1)}, f32[8,3072]{1,0:T(8,128)}, bf16[640,768]{1,0:T(8,128)(2,1)}, bf16[384,3072]{1,0:T(8,128)(2,1)}, bf16[384...) custom-call(s32[2]{0:T(128)} %pad_add_fusion.word_ref, bf16[640,768]{1,0:T(8,128)(2,1)} %bitcast.170, ...), custom_call_target="tpu_custom_call" | custom-call | flops 18119393280 | bytes 25165824 | tf_op jit(solution)/shard_map/expert_0/expert_0/pallas_call | solution.py:735
  275.9 6.3 %all-to-all-start.4 = ((bf16[8,80,768]{2,1,0:T(8,128)(2,1)}), bf16[8,80,768]{2,1,0:T(8,128)(2,1)S(1)}, u32[]{:S(2)}, u32[]{:S(2)}) async-start(bf16[8,80,768]{2,1,0:T(8,128)(2,1)} %bitcast.173), calls=%async_computation.4 | async-start | bytes 1966080 | tf_op jit(solution)/shard_map/rows_back_0/all_to_all | solution.py:793
  282.2 31.1 %expert_1.1 = (bf16[8,2,80,768]{3,2,1,0:T(8,128)(2,1)}, f32[8,3072]{1,0:T(8,128)}, bf16[640,768]{1,0:T(8,128)(2,1)}, bf16[384,3072]{1,0:T(8,128)(2,1)}, bf16[384...) custom-call(s32[2]{0:T(128)} %pad_add_fusion.word_ref, ...), custom_call_target="tpu_custom_call", output_to_operand_aliasing={{0}: (12, {})} | custom-call | flops 18119393280 | bytes 25165824 | tf_op jit(solution)/shard_map/expert_1/expert_1/pallas_call | solution.py:735
  313.3 6.0 %all-to-all-start.5 = ((bf16[8,80,768]{2,1,0:T(8,128)(2,1)}), bf16[8,80,768]{2,1,0:T(8,128)(2,1)}, u32[]{:S(2)}, u32[]{:S(2)}) async-start(bf16[8,80,768]{2,1,0:T(8,128)(2,1)} %bitcast.169), calls=%async_computation.5 | async-start | bytes 1966080 | tf_op jit(solution)/shard_map/rows_back_1/all_to_all | solution.py:793
  333.8 3.0 fusion.39
  336.8 6.1 %all-to-all-done.5 = bf16[8,80,768]{2,1,0:T(8,128)(2,1)} async-done(((bf16[8,80,768]{2,1,0:T(8,128)(2,1)}), bf16[8,80,768]{2,1,0:T(8,128)(2,1)}, u32[]{:S(2)}, u32[]{:S(2)}) %all-to-all-start.5) | async-done | bytes 983072 | tf_op jit(solution)/shard_map/rows_back_1/all_to_all | solution.py:793
  343.0 4.8 all-to-all-start.3
  347.8 4.2 fusion.35
  359.0 3.1 fusion.71
  371.5 4.8 cross_backward_0.1
  376.2 7.8 %collective-permute-start.17 = (bf16[1024,256]{1,0:T(8,128)(2,1)}, bf16[1024,256]{1,0:T(8,128)(2,1)S(1)}, u32[]{:S(2)}, u32[]{:S(2)}) collective-permute-start(bf16[1024,256]{1,0:T(8,128)(2,1)} %get-tuple-element.61), channel_id=1, source_target_pairs={{0,2},{2,0},{1,3},{3,1},{4,6},{6,4},{5,7},{7,5},{8,10},{10,8},{9,1... | collective-permute-start | bytes 1572872 | tf_op jit(solution)/shard_map/far_back_0/ppermute | solution.py:785
  384.1 4.6 cross_backward_1.1
  388.7 5.1 cross_backward_2.1
  393.8 3.6 convolution_convert_fusion.7
  397.4 29.8 %collective-permute-done.17.far_ref = bf16[1024,256]{1,0:T(8,128)(2,1)S(1)} collective-permute-done((bf16[1024,256]{1,0:T(8,128)(2,1)}, bf16[1024,256]{1,0:T(8,128)(2,1)S(1)}, u32[]{:S(2)}, u32[]{:S(2)}) %collective-permute-start.17) | collective-permute-done | bytes 524320 | tf_op jit(solution)/shard_map/far_back_0/ppermute | solution.py:785
  428.6 9.8 %self_backward_0.1.rest_0_ = bf16[1280,1152]{1,0:T(8,128)(2,1)} custom-call(bf16[1280,1152]{1,0:T(8,128)(2,1)} %copy-done, bf16[1280,1152]{1,0:T(8,128)(2,1)} %copy-done, bf16[1280,1152]{1,0:T(8,128)(2,1)} %copy-done, bf16[1280,384]{1,0:T(8,128)(2,1)} %convolution_convert_fusion.2.g_ref, bf16[1280,384]{1,0:T(8,128)(2,1)} %get-tuple-element.48.c_ref, ...), custom_call_target="tpu_custom_call" | custom-call | flops 3355443200 | bytes 5242880 | tf_op jit(solution)/shard_map/self_backward_0/pallas_call | solution.py:616
  438.5 3.8 convolution_convert_fusion.6
  443.1 6.1 %all-to-all-start.6 = ((bf16[8,96,384]{2,1,0:T(8,128)(2,1)}), bf16[8,96,384]{2,1,0:T(8,128)(2,1)S(1)}, u32[]{:S(2)}, u32[]{:S(2)}) async-start(bf16[8,96,384]{2,1,0:T(8,128)(2,1)} %bitcast.25), calls=%async_computation.6 | async-start | bytes 1179648 | tf_op jit(solution)/shard_map/out_sum/all_to_all | solution.py:793
  449.2 9.8 %self_backward_1.1.rest_0_ = bf16[1280,1152]{1,0:T(8,128)(2,1)} custom-call(bf16[1280,1152]{1,0:T(8,128)(2,1)} %copy-done, bf16[1280,1152]{1,0:T(8,128)(2,1)} %copy-done, bf16[1280,1152]{1,0:T(8,128)(2,1)} %copy-done, bf16[1280,384]{1,0:T(8,128)(2,1)} %convolution_convert_fusion.2.g_ref, ...), custom_call_target="tpu_custom_call", output_to_operand_aliasing={{}: (8, {})} | custom-call | flops 3355443200 | bytes 5242880 | tf_op jit(solution)/shard_map/self_backward_1/pallas_call | solution.py:616
  459.1 3.8 convolution_convert_fusion.5
  463.7 10.1 %self_backward_2.1 = bf16[1280,1152]{1,0:T(8,128)(2,1)} custom-call(bf16[1280,1152]{1,0:T(8,128)(2,1)} %copy-done, bf16[1280,1152]{1,0:T(8,128)(2,1)} %copy-done, bf16[1280,1152]{1,0:T(8,128)(2,1)} %copy-done, bf16[1280,384]{1,0:T(8,128)(2,1)} %convolution_convert_fusion.2.g_ref, ...), custom_call_target="tpu_custom_call", output_to_operand_aliasing={{}: (8, {})} | custom-call | flops 3355443200 | bytes 5242880 | tf_op jit(solution)/shard_map/self_backward_2/pallas_call | solution.py:616
  473.8 3.8 convolution_convert_fusion.4
  477.6 6.0 %all-to-all-start.9 = ((bf16[8,96,384]{2,1,0:T(8,128)(2,1)}), bf16[8,96,384]{2,1,0:T(8,128)(2,1)S(1)}, u32[]{:S(2)}, u32[]{:S(2)}) async-start(bf16[8,96,384]{2,1,0:T(8,128)(2,1)} %bitcast.183), calls=%async_computation.9 | async-start | bytes 1179648 | tf_op jit(solution)/shard_map/qkv_sum_2/all_to_all | solution.py:793
  483.6 3.2 fusion.72
  491.5 7.0 %all-to-all-done.9 = bf16[8,96,384]{2,1,0:T(8,128)(2,1)S(1)} async-done(((bf16[8,96,384]{2,1,0:T(8,128)(2,1)}), bf16[8,96,384]{2,1,0:T(8,128)(2,1)S(1)}, u32[]{:S(2)}, u32[]{:S(2)}) %all-to-all-start.9) | async-done | bytes 589856 | tf_op jit(solution)/shard_map/qkv_sum_2/all_to_all | solution.py:793
  498.5 4.2 all-to-all-start.8
  502.7 6.5 %convolution_convert_fusion.1 = bf16[1280,768]{1,0:T(8,128)(2,1)} fusion(bf16[1280,1152]{1,0:T(8,128)(2,1)} %self_backward_2.1, bf16[768,1152]{1,0:T(8,128)(2,1)} %all-gather.2.cloned.1.call-done), kind=kOutput, calls=%fused_computation.24 | convolution fusion | flops 2265907200 | bytes 6684672 | tf_op jit(solution)/shard_map/dot_general | solution.py:1023
  517.3 4.7 all-to-all-start.7
  522.3 3.9 fusion.27
  527.6 11.0 %all-to-all-done.7 = bf16[8,96,384]{2,1,0:T(8,128)(2,1)} async-done(((bf16[8,96,384]{2,1,0:T(8,128)(2,1)}), bf16[8,96,384]{2,1,0:T(8,128)(2,1)}, u32[]{:S(2)}, u32[]{:S(2)}) %all-to-all-start.7) | async-done | bytes 589856 | tf_op jit(solution)/shard_map/qkv_sum_0/all_to_all | solution.py:793
  541.0 3.8 fusion.29
  559.3 3.9 fusion.14
  564.0 5.2 all-to-all-start.10
  569.1 6.6 %all-to-all-done.10 = f32[8,4,96]{2,1,0:T(4,128)S(1)} async-done(((f32[8,4,96]{2,1,0:T(4,128)}), f32[8,4,96]{2,1,0:T(4,128)S(1)}, u32[]{:S(2)}, u32[]{:S(2)}) %all-to-all-start.10) | async-done | bytes 12320 | tf_op jit(solution)/shard_map/all_to_all | solution.py:793
  576.9 4.9 fusion.13
  (264 shorter events, 118.8 us)
Async XLA Ops:
  7.2 105.1 %all-gather.2.cloned.1.call-start = ((), (), s32[]{:S(2)}) async-start(), calls=%async_computation.11 | async-start | bytes 1990656 | tf_op jit(solution)/shard_map/gather_qkv/all_gather | solution.py:841
  15.8 186.4 %all-to-all-start.1 = ((bf16[8,2,80,768]{3,2,1,0:T(8,128)(2,1)}), bf16[8,2,80,768]{3,2,1,0:T(8,128)(2,1)}, u32[]{:S(2)}, u32[]{:S(2)}) async-start(bf16[8,2,80,768]{3,2,1,0:T(8,128)(2,1)} %pad_maximum_fusion.2), calls=%async_computation.1 | async-start | bytes 3932160 | tf_op jit(solution)/shard_map/cot_out/all_to_all | solution.py:793
  23.2 139.8 %collective-permute-start.4 = (bf16[2,192,3072]{2,1,0:T(8,128)(2,1)}, bf16[2,192,3072]{2,1,0:T(8,128)(2,1)}, u32[]{:S(2)}, u32[]{:S(2)}) collective-permute-start(bf16[2,192,3072]{2,1,0:T(8,128)(2,1)} %refs_3_.3), channel_id=1, source_target_pairs={{0,2},{2,0},{1,3},{3,1},{4,6},{6,4},{5,7},{7,5},{8,10},{10,8},{9,1... | collective-permute-start | bytes 7077896 | tf_op jit(solution)/shard_map/up_ctx/ppermute | solution.py:785
  25.9 84.3 %copy-start.24 = (f32[768]{0:T(1024)}, f32[768]{0:T(1024)S(1)}, u32[]{:S(2)}) copy-start(f32[768]{0:T(1024)S(1)} %get-tuple-element.84) | copy-start | bytes 9220
  118.3 19.2 %collective-permute-start.2 = (bf16[1024,256]{1,0:T(8,128)(2,1)}, bf16[1024,256]{1,0:T(8,128)(2,1)}, u32[]{:S(2)}, u32[]{:S(2)}) collective-permute-start(bf16[1024,256]{1,0:T(8,128)(2,1)} %get-tuple-element.89), channel_id=1, source_target_pairs={{0,2},{2,0},{1,3},{3,1},{4,6},{6,4},{5,7},{7,5},{8,10},{10,8},{9,1... | collective-permute-start | bytes 1572872 | tf_op jit(solution)/shard_map/far_0/ppermute | solution.py:785
  119.7 24.9 %collective-permute-start.1 = (bf16[1024,256]{1,0:T(8,128)(2,1)}, bf16[1024,256]{1,0:T(8,128)(2,1)}, u32[]{:S(2)}, u32[]{:S(2)}) collective-permute-start(bf16[1024,256]{1,0:T(8,128)(2,1)} %get-tuple-element.90), channel_id=1, source_target_pairs={{0,2},{2,0},{1,3},{3,1},{4,6},{6,4},{5,7},{7,5},{8,10},{10,8},{9,1... | collective-permute-start | bytes 1572872 | tf_op jit(solution)/shard_map/far_1/ppermute | solution.py:785
  120.3 35.6 %collective-permute-start = (bf16[1024,256]{1,0:T(8,128)(2,1)}, bf16[1024,256]{1,0:T(8,128)(2,1)}, u32[]{:S(2)}, u32[]{:S(2)}) collective-permute-start(bf16[1024,256]{1,0:T(8,128)(2,1)} %get-tuple-element.91), channel_id=1, source_target_pairs={{0,2},{2,0},{1,3},{3,1},{4,6},{6,4},{5,7},{7,5},{8,10},{10,8},{9,1... | collective-permute-start | bytes 1572872 | tf_op jit(solution)/shard_map/far_2/ppermute | solution.py:785
  137.5 62.3 %collective-permute-start.7 = (bf16[2,768,768]{2,1,0:T(8,128)(2,1)}, bf16[2,768,768]{2,1,0:T(8,128)(2,1)}, u32[]{:S(2)}, u32[]{:S(2)}) collective-permute-start(bf16[2,768,768]{2,1,0:T(8,128)(2,1)} %refs_7_.3), channel_id=1, source_target_pairs={{0,2},{2,0},{1,3},{3,1},{4,6},{6,4},{5,7},{7,5},{8,10},{10,8},{9,1... | collective-permute-start | bytes 7077896 | tf_op jit(solution)/shard_map/down_ctx/ppermute | solution.py:785
  162.3 2.6 collective-permute-start.3
  162.4 82.4 %collective-permute-start.6 = (bf16[2,192,3072]{2,1,0:T(8,128)(2,1)}, bf16[2,192,3072]{2,1,0:T(8,128)(2,1)}, u32[]{:S(2)}, u32[]{:S(2)}) collective-permute-start(bf16[2,192,3072]{2,1,0:T(8,128)(2,1)} %refs_3_.3), channel_id=1, source_target_pairs={{0,1},{1,0},{2,3},{3,2},{4,5},{5,4},{6,7},{7,6},{8,9},{9,8},{10,11... | collective-permute-start | bytes 7077896 | tf_op jit(solution)/shard_map/up_tp/ppermute | solution.py:785
  162.9 81.9 %collective-permute-start.9 = (bf16[2,768,768]{2,1,0:T(8,128)(2,1)}, bf16[2,768,768]{2,1,0:T(8,128)(2,1)}, u32[]{:S(2)}, u32[]{:S(2)}) collective-permute-start(bf16[2,768,768]{2,1,0:T(8,128)(2,1)} %refs_7_.3), channel_id=1, source_target_pairs={{0,1},{1,0},{2,3},{3,2},{4,5},{5,4},{6,7},{7,6},{8,9},{9,8},{10,11... | collective-permute-start | bytes 7077896 | tf_op jit(solution)/shard_map/down_tp/ppermute | solution.py:785
  163.0 81.8 %collective-permute-start.5 = (bf16[2,192,3072]{2,1,0:T(8,128)(2,1)}, bf16[2,192,3072]{2,1,0:T(8,128)(2,1)}, u32[]{:S(2)}, u32[]{:S(2)}) collective-permute-start(bf16[2,192,3072]{2,1,0:T(8,128)(2,1)} %collective-permute-done.4.refs_2_), channel_id=1, source_target_pairs={{0,1},{1,0},{2,3},{3,2},{4,5},{5,4},{6,7},{7,6},{8,9},{9,8},{10,11... | collective-permute-start | bytes 7077896 | tf_op jit(solution)/shard_map/up_tp/ppermute | solution.py:785
  166.8 33.4 %copy-start.3 = (f32[640,768]{1,0:T(8,128)}, f32[640,768]{1,0:T(8,128)S(1)}, u32[]{:S(2)}) copy-start(f32[640,768]{1,0:T(8,128)S(1)} %get-tuple-element.113) | copy-start | bytes 5898244
  166.9 33.3 %copy-start.26 = (f32[640]{0:T(1024)}, f32[640]{0:T(1024)S(1)}, u32[]{:S(2)}) copy-start(f32[640]{0:T(1024)S(1)} %broadcast_multiply_fusion.5) | copy-start | bytes 7684
  167.3 33.0 %copy-start.50 = (pred[640]{0:T(1024)(128)(4,1)S(1)}, pred[640]{0:T(1024)(128)(4,1)}, u32[]{:S(2)}) copy-start(pred[640]{0:T(1024)(128)(4,1)} %copy-done.49) | copy-start | bytes 1924
  199.8 45.0 %collective-permute-start.8 = (bf16[2,768,768]{2,1,0:T(8,128)(2,1)}, bf16[2,768,768]{2,1,0:T(8,128)(2,1)}, u32[]{:S(2)}, u32[]{:S(2)}) collective-permute-start(bf16[2,768,768]{2,1,0:T(8,128)(2,1)} %collective-permute-done.7.refs_6_), channel_id=1, source_target_pairs={{0,1},{1,0},{2,3},{3,2},{4,5},{5,4},{6,7},{7,6},{8,9},{9,8},{10,11... | collective-permute-start | bytes 7077896 | tf_op jit(solution)/shard_map/down_tp/ppermute | solution.py:785
  202.2 28.8 %all-to-all-start.2 = ((bf16[8,80,768]{2,1,0:T(8,128)(2,1)}), bf16[8,80,768]{2,1,0:T(8,128)(2,1)S(1)}, u32[]{:S(2)}, u32[]{:S(2)}) async-start(bf16[8,80,768]{2,1,0:T(8,128)(2,1)} %bitcast.172), calls=%async_computation.2 | async-start | bytes 1966080 | tf_op jit(solution)/shard_map/rows_out_0/all_to_all | solution.py:793
  207.2 3.9 collective-permute-start.10
  211.1 1.5 collective-permute-start.11
  212.6 1.5 collective-permute-start.12
  231.0 44.9 %all-to-all-start = ((bf16[8,80,768]{2,1,0:T(8,128)(2,1)}), bf16[8,80,768]{2,1,0:T(8,128)(2,1)}, u32[]{:S(2)}, u32[]{:S(2)}) async-start(bf16[8,80,768]{2,1,0:T(8,128)(2,1)} %bitcast.171), calls=%async_computation | async-start | bytes 1966080 | tf_op jit(solution)/shard_map/rows_out_1/all_to_all | solution.py:793
  275.9 37.3 %all-to-all-start.4 = ((bf16[8,80,768]{2,1,0:T(8,128)(2,1)}), bf16[8,80,768]{2,1,0:T(8,128)(2,1)S(1)}, u32[]{:S(2)}, u32[]{:S(2)}) async-start(bf16[8,80,768]{2,1,0:T(8,128)(2,1)} %bitcast.173), calls=%async_computation.4 | async-start | bytes 1966080 | tf_op jit(solution)/shard_map/rows_back_0/all_to_all | solution.py:793
  313.3 29.7 %all-to-all-start.5 = ((bf16[8,80,768]{2,1,0:T(8,128)(2,1)}), bf16[8,80,768]{2,1,0:T(8,128)(2,1)}, u32[]{:S(2)}, u32[]{:S(2)}) async-start(bf16[8,80,768]{2,1,0:T(8,128)(2,1)} %bitcast.169), calls=%async_computation.5 | async-start | bytes 1966080 | tf_op jit(solution)/shard_map/rows_back_1/all_to_all | solution.py:793
  319.3 1.5 collective-permute-start.26
  322.3 5.2 collective-permute-start.27
  323.9 35.1 %collective-permute-start.28 = (bf16[2,768,768]{2,1,0:T(8,128)(2,1)}, bf16[2,768,768]{2,1,0:T(8,128)(2,1)}, u32[]{:S(2)}, u32[]{:S(2)}) collective-permute-start(bf16[2,768,768]{2,1,0:T(8,128)(2,1)} %get-tuple-element.69), channel_id=1, source_target_pairs={{0,1},{1,0},{2,3},{3,2},{4,5},{5,4},{6,7},{7,6},{8,9},{9,8},{10,11... | collective-permute-start | bytes 7077896 | tf_op jit(solution)/shard_map/down_grad_tp_0/ppermute | solution.py:785
  323.9 159.7 %collective-permute-start.30 = (bf16[2,768,768]{2,1,0:T(8,128)(2,1)}, bf16[2,768,768]{2,1,0:T(8,128)(2,1)}, u32[]{:S(2)}, u32[]{:S(2)}) collective-permute-start(bf16[2,768,768]{2,1,0:T(8,128)(2,1)} %get-tuple-element.71), channel_id=1, source_target_pairs={{0,1},{1,0},{2,3},{3,2},{4,5},{5,4},{6,7},{7,6},{8,9},{9,8},{10,11... | collective-permute-start | bytes 7077896 | tf_op jit(solution)/shard_map/down_grad_tp_1/ppermute | solution.py:785
  324.4 39.1 %collective-permute-start.22 = (bf16[2,192,3072]{2,1,0:T(8,128)(2,1)}, bf16[2,192,3072]{2,1,0:T(8,128)(2,1)}, u32[]{:S(2)}, u32[]{:S(2)}) collective-permute-start(bf16[2,192,3072]{2,1,0:T(8,128)(2,1)} %bitcast.189), channel_id=1, source_target_pairs={{0,1},{1,0},{2,3},{3,2},{4,5},{5,4},{6,7},{7,6},{8,9},{9,8},{10,11... | collective-permute-start | bytes 7077896 | tf_op jit(solution)/shard_map/up_grad_tp_0/ppermute | solution.py:785
  324.4 162.4 %collective-permute-start.24 = (bf16[2,192,3072]{2,1,0:T(8,128)(2,1)}, bf16[2,192,3072]{2,1,0:T(8,128)(2,1)}, u32[]{:S(2)}, u32[]{:S(2)}) collective-permute-start(bf16[2,192,3072]{2,1,0:T(8,128)(2,1)} %bitcast.188), channel_id=1, source_target_pairs={{0,1},{1,0},{2,3},{3,2},{4,5},{5,4},{6,7},{7,6},{8,9},{9,8},{10,11... | collective-permute-start | bytes 7077896 | tf_op jit(solution)/shard_map/up_grad_tp_1/ppermute | solution.py:785
  343.0 100.1 %all-to-all-start.3 = ((bf16[8,2,80,768]{3,2,1,0:T(8,128)(2,1)}), bf16[8,2,80,768]{3,2,1,0:T(8,128)(2,1)}, u32[]{:S(2)}, u32[]{:S(2)}) async-start(bf16[8,2,80,768]{3,2,1,0:T(8,128)(2,1)} %get-tuple-element.52), calls=%async_computation.3 | async-start | bytes 3932160 | tf_op jit(solution)/shard_map/output_back/all_to_all | solution.py:793
  352.2 3.5 collective-permute-start.20
  355.7 11.2 %collective-permute-start.14 = (bf16[640,768]{1,0:T(8,128)(2,1)S(1)}, bf16[640,768]{1,0:T(8,128)(2,1)}, u32[]{:S(2)}, u32[]{:S(2)}) collective-permute-start(bf16[640,768]{1,0:T(8,128)(2,1)S(1)} %get-tuple-element.88), channel_id=1, source_target_pairs={{0,1},{1,0},{2,3},{3,2},{4,5},{5,4},{6,7},{7,6},{8,9},{9,8},{10,11... | collective-permute-start | bytes 2949128 | tf_op jit(solution)/shard_map/attended_grad_tp/ppermute | solution.py:785
  362.1 177.8 %collective-permute-start.29 = (bf16[768,768]{1,0:T(8,128)(2,1)}, bf16[768,768]{1,0:T(8,128)(2,1)}, u32[]{:S(2)}, u32[]{:S(2)}) collective-permute-start(bf16[768,768]{1,0:T(8,128)(2,1)} %fusion.71), channel_id=1, source_target_pairs={{0,2},{2,0},{1,3},{3,1},{4,6},{6,4},{5,7},{7,5},{8,10},{10,8},{9,1... | collective-permute-start | bytes 3538952 | tf_op jit(solution)/shard_map/grad_ctx_0_1/ppermute | solution.py:785
  366.2 155.8 %collective-permute-start.23 = (bf16[192,3072]{1,0:T(8,128)(2,1)}, bf16[192,3072]{1,0:T(8,128)(2,1)}, u32[]{:S(2)}, u32[]{:S(2)}) collective-permute-start(bf16[192,3072]{1,0:T(8,128)(2,1)} %fusion.25), channel_id=1, source_target_pairs={{0,2},{2,0},{1,3},{3,1},{4,6},{6,4},{5,7},{7,5},{8,10},{10,8},{9,1... | collective-permute-start | bytes 3538952 | tf_op jit(solution)/shard_map/grad_ctx_0_0/ppermute | solution.py:785
  376.2 50.9 %collective-permute-start.17 = (bf16[1024,256]{1,0:T(8,128)(2,1)}, bf16[1024,256]{1,0:T(8,128)(2,1)S(1)}, u32[]{:S(2)}, u32[]{:S(2)}) collective-permute-start(bf16[1024,256]{1,0:T(8,128)(2,1)} %get-tuple-element.61), channel_id=1, source_target_pairs={{0,2},{2,0},{1,3},{3,1},{4,6},{6,4},{5,7},{7,5},{8,10},{10,8},{9,1... | collective-permute-start | bytes 1572872 | tf_op jit(solution)/shard_map/far_back_0/ppermute | solution.py:785
  427.2 15.1 %collective-permute-start.16 = (bf16[1024,256]{1,0:T(8,128)(2,1)}, bf16[1024,256]{1,0:T(8,128)(2,1)S(1)}, u32[]{:S(2)}, u32[]{:S(2)}) collective-permute-start(bf16[1024,256]{1,0:T(8,128)(2,1)} %get-tuple-element.59), channel_id=1, source_target_pairs={{0,2},{2,0},{1,3},{3,1},{4,6},{6,4},{5,7},{7,5},{8,10},{10,8},{9,1... | collective-permute-start | bytes 1572872 | tf_op jit(solution)/shard_map/far_back_1/ppermute | solution.py:785
  442.3 20.6 %collective-permute-start.15 = (bf16[1024,256]{1,0:T(8,128)(2,1)}, bf16[1024,256]{1,0:T(8,128)(2,1)S(1)}, u32[]{:S(2)}, u32[]{:S(2)}) collective-permute-start(bf16[1024,256]{1,0:T(8,128)(2,1)} %get-tuple-element.57), channel_id=1, source_target_pairs={{0,2},{2,0},{1,3},{3,1},{4,6},{6,4},{5,7},{7,5},{8,10},{10,8},{9,1... | collective-permute-start | bytes 1572872 | tf_op jit(solution)/shard_map/far_back_2/ppermute | solution.py:785
  443.1 34.5 %all-to-all-start.6 = ((bf16[8,96,384]{2,1,0:T(8,128)(2,1)}), bf16[8,96,384]{2,1,0:T(8,128)(2,1)S(1)}, u32[]{:S(2)}, u32[]{:S(2)}) async-start(bf16[8,96,384]{2,1,0:T(8,128)(2,1)} %bitcast.25), calls=%async_computation.6 | async-start | bytes 1179648 | tf_op jit(solution)/shard_map/out_sum/all_to_all | solution.py:793
  477.6 20.9 %all-to-all-start.9 = ((bf16[8,96,384]{2,1,0:T(8,128)(2,1)}), bf16[8,96,384]{2,1,0:T(8,128)(2,1)S(1)}, u32[]{:S(2)}, u32[]{:S(2)}) async-start(bf16[8,96,384]{2,1,0:T(8,128)(2,1)} %bitcast.183), calls=%async_computation.9 | async-start | bytes 1179648 | tf_op jit(solution)/shard_map/qkv_sum_2/all_to_all | solution.py:793
  489.5 56.7 %collective-permute-start.31 = (bf16[768,768]{1,0:T(8,128)(2,1)}, bf16[768,768]{1,0:T(8,128)(2,1)}, u32[]{:S(2)}, u32[]{:S(2)}) collective-permute-start(bf16[768,768]{1,0:T(8,128)(2,1)} %fusion.72), channel_id=1, source_target_pairs={{0,2},{2,0},{1,3},{3,1},{4,6},{6,4},{5,7},{7,5},{8,10},{10,8},{9,1... | collective-permute-start | bytes 3538952 | tf_op jit(solution)/shard_map/grad_ctx_1_1/ppermute | solution.py:785
  490.7 61.2 %collective-permute-start.25 = (bf16[192,3072]{1,0:T(8,128)(2,1)}, bf16[192,3072]{1,0:T(8,128)(2,1)}, u32[]{:S(2)}, u32[]{:S(2)}) collective-permute-start(bf16[192,3072]{1,0:T(8,128)(2,1)} %fusion.22), channel_id=1, source_target_pairs={{0,2},{2,0},{1,3},{3,1},{4,6},{6,4},{5,7},{7,5},{8,10},{10,8},{9,1... | collective-permute-start | bytes 3538952 | tf_op jit(solution)/shard_map/grad_ctx_1_0/ppermute | solution.py:785
  498.5 18.8 %all-to-all-start.8 = ((bf16[8,96,384]{2,1,0:T(8,128)(2,1)}), bf16[8,96,384]{2,1,0:T(8,128)(2,1)}, u32[]{:S(2)}, u32[]{:S(2)}) async-start(bf16[8,96,384]{2,1,0:T(8,128)(2,1)} %bitcast.182), calls=%async_computation.8 | async-start | bytes 1179648 | tf_op jit(solution)/shard_map/qkv_sum_1/all_to_all | solution.py:793
  509.2 50.1 %collective-permute-start.18 = (bf16[1280,768]{1,0:T(8,128)(2,1)}, bf16[1280,768]{1,0:T(8,128)(2,1)}, u32[]{:S(2)}, u32[]{:S(2)}) collective-permute-start(bf16[1280,768]{1,0:T(8,128)(2,1)} %convolution_convert_fusion.1), channel_id=1, source_target_pairs={{0,1},{1,0},{2,3},{3,2},{4,5},{5,4},{6,7},{7,6},{8,9},{9,8},{10,11... | collective-permute-start | bytes 5898248 | tf_op jit(solution)/shard_map/first_tp/ppermute | solution.py:785
  517.3 21.3 %all-to-all-start.7 = ((bf16[8,96,384]{2,1,0:T(8,128)(2,1)}), bf16[8,96,384]{2,1,0:T(8,128)(2,1)}, u32[]{:S(2)}, u32[]{:S(2)}) async-start(bf16[8,96,384]{2,1,0:T(8,128)(2,1)} %bitcast.181), calls=%async_computation.7 | async-start | bytes 1179648 | tf_op jit(solution)/shard_map/qkv_sum_0/all_to_all | solution.py:793
  522.0 35.0 %collective-permute-start.13 = (bf16[640,768]{1,0:T(8,128)(2,1)}, bf16[640,768]{1,0:T(8,128)(2,1)}, u32[]{:S(2)}, u32[]{:S(2)}) collective-permute-start(bf16[640,768]{1,0:T(8,128)(2,1)} %get-tuple-element.115), channel_id=1, source_target_pairs={{0,1},{1,0},{2,3},{3,2},{4,5},{5,4},{6,7},{7,6},{8,9},{9,8},{10,11... | collective-permute-start | bytes 2949128 | tf_op jit(solution)/shard_map/mixed_tp/ppermute | solution.py:785
  539.9 5.2 collective-permute-start.19
  564.0 11.7 %all-to-all-start.10 = ((f32[8,4,96]{2,1,0:T(4,128)}), f32[8,4,96]{2,1,0:T(4,128)S(1)}, u32[]{:S(2)}, u32[]{:S(2)}) async-start(f32[8,4,96]{2,1,0:T(4,128)} %maximum_bitcast_fusion), calls=%async_computation.10 | async-start | bytes 32768 | tf_op jit(solution)/shard_map/all_to_all | solution.py:793
  575.7 6.1 %collective-permute-start.21 = (f32[4,96]{1,0:T(4,128)S(1)}, f32[4,96]{1,0:T(4,128)S(1)}, u32[]{:S(2)}, u32[]{:S(2)}) collective-permute-start(f32[4,96]{1,0:T(4,128)S(1)} %reduce_sum.179), channel_id=1, source_target_pairs={{0,2},{2,0},{1,3},{3,1},{4,6},{6,4},{5,7},{7,5},{8,10},{10,8},{9,1... | collective-permute-start | bytes 4616 | tf_op jit(solution)/shard_map/ppermute | solution.py:785
  (48 other events, 288.2 us)
Sparse Core Ops, SparseCore 0:
  10.8 75.9 all-gather.1
